TPU v7x, 32 devices: a whole 2x2x4 slice. The times are simulated.
32 devices in a mesh: fft: 16 (over z, x, core), grp: 2 (over y).
Axes of the slice: x: 2, y: 2, z: 4, core: 2. Of those that a mesh axis runs over, the one named last changes fastest.
Arguments:
- limbs_a: int32 [4096, 8192], P(('fft', 'grp')), may hold values from -128 to 127
- limbs_b: int32 [4096, 8192], P(('fft', 'grp')), may hold values from -128 to 127
Outputs:
- product: float32 [4096, 16384], P(('fft', 'grp'))
All inputs are finite; a program needn't handle non-finite values.
Results may differ from a plain program's by a relative error of at most 0.000098.
Values sent between devices are 32-bit elements; how exact they have to be, the bound alone decides.
No kernel may reach another device: no remote copies, remote signals or barrier semaphores. Data moves between devices by JAX's collectives and lax.ppermute only.
A program may use at most 192 MiB of HBM per device.

v0:
```python
import math

import jax
import jax.numpy as jnp
from jax import lax
from jax.sharding import PartitionSpec as P

ROWS = 16384
COLS = 4096


HIGHEST = lax.Precision.HIGHEST
TWO_PI = 2.0 * math.pi
DIGIT_VAR = 5461.25


def padded_2(value, sides, width):
    for axis, dim in sides:
        size, length = (lax.axis_size(axis), value.shape[dim])
        up = [(i, (i + 1) % size) for i in range(size - 1)]
        down = [(j, i) for i, j in up]
        last = lax.slice_in_dim(value, length - width, length, axis=dim)
        first = lax.slice_in_dim(value, 0, width, axis=dim)
        before = lax.ppermute(last, axis, up)
        after = lax.ppermute(first, axis, down)
        value = jnp.concatenate([before, value, after], axis=dim)
    return value


def split_length(length):
    bit_count = length.bit_length() - 1
    outer_len = 2 ** (bit_count // 2)
    return (outer_len, length // outer_len)


def angle_pair(phases, phase_sign, modulus):
    angles = phases.astype(jnp.float32) * (phase_sign * TWO_PI / modulus)
    return (jnp.cos(angles), jnp.sin(angles))


def dft_table(modulus, phase_sign, row_total):
    row_ids = lax.broadcasted_iota(jnp.int32, (row_total, modulus), 0)
    col_ids = lax.broadcasted_iota(jnp.int32, (row_total, modulus), 1)
    return angle_pair(row_ids * col_ids % modulus, phase_sign, modulus)


def inner_twiddle(outer_len, inner_len, phase_sign):
    modulus = outer_len * inner_len
    row_ids = lax.broadcasted_iota(jnp.int32, (outer_len, inner_len), 0)
    col_ids = lax.broadcasted_iota(jnp.int32, (outer_len, inner_len), 1)
    return angle_pair(row_ids * col_ids % modulus, phase_sign, modulus)


def complex_einsum(pattern, left_side, right_side):
    real_part = jnp.einsum(pattern, left_side[0], right_side[0], precision=HIGHEST) - jnp.einsum(
        pattern, left_side[1], right_side[1], precision=HIGHEST
    )
    imag_part = jnp.einsum(pattern, left_side[0], right_side[1], precision=HIGHEST) + jnp.einsum(
        pattern, left_side[1], right_side[0], precision=HIGHEST
    )
    return (real_part, imag_part)


def complex_times(left_side, right_side):
    real_part = left_side[0] * right_side[0] - left_side[1] * right_side[1]
    imag_part = left_side[0] * right_side[1] + left_side[1] * right_side[0]
    return (real_part, imag_part)


def transform_last(values, length, phase_sign, first_col, twiddle_after, real_only):
    outer_len, inner_len = split_length(length)
    total = ROWS * COLS
    row_count = values[0].shape[0]
    used_rows = values[0].shape[1] // inner_len
    shaped = (
        values[0].reshape(row_count, used_rows, inner_len),
        values[1].reshape(row_count, used_rows, inner_len),
    )
    shape_a = (row_count, used_rows, outer_len)
    cols_a = lax.broadcasted_iota(jnp.int32, shape_a, 0) + first_col
    lead_a = lax.broadcasted_iota(jnp.int32, shape_a, 1)
    freq_a = lax.broadcasted_iota(jnp.int32, shape_a, 2)
    base_a = lead_a * freq_a % outer_len * (total // outer_len)
    if twiddle_after:
        extra_a = cols_a * freq_a % total
    else:
        extra_a = cols_a * lead_a * inner_len % total
    table_a = angle_pair((base_a + extra_a) % total, phase_sign, total)
    mixed_terms = complex_einsum("phl,phk->pkl", shaped, table_a)
    turned = complex_times(mixed_terms, inner_twiddle(outer_len, inner_len, phase_sign))
    shape_b = (row_count, inner_len, inner_len)
    cols_b = lax.broadcasted_iota(jnp.int32, shape_b, 0) + first_col
    lane_b = lax.broadcasted_iota(jnp.int32, shape_b, 1)
    freq_b = lax.broadcasted_iota(jnp.int32, shape_b, 2)
    base_b = lane_b * freq_b % inner_len * (total // inner_len)
    if twiddle_after:
        extra_b = cols_b * freq_b * outer_len % total
    else:
        extra_b = cols_b * lane_b % total
    table_b = angle_pair((base_b + extra_b) % total, phase_sign, total)
    if real_only:
        real_part = jnp.einsum(
            "pkl,plh->phk", turned[0], table_b[0], precision=HIGHEST
        ) - jnp.einsum("pkl,plh->phk", turned[1], table_b[1], precision=HIGHEST)
        return real_part.reshape(row_count, length)
    result = complex_einsum("pkl,plh->phk", turned, table_b)
    return (result[0].reshape(row_count, length), result[1].reshape(row_count, length))


def transform_first(values, length, phase_sign):
    outer_len, inner_len = split_length(length)
    trailing = values[0].shape[1]
    shaped = (
        values[0].reshape(outer_len, inner_len, trailing),
        values[1].reshape(outer_len, inner_len, trailing),
    )
    mixed_terms = complex_einsum("hlq,hk->klq", shaped, dft_table(outer_len, phase_sign, outer_len))
    twiddle = inner_twiddle(outer_len, inner_len, phase_sign)
    turned = complex_times(mixed_terms, (twiddle[0][:, :, None], twiddle[1][:, :, None]))
    result = complex_einsum("klq,lh->hkq", turned, dft_table(inner_len, phase_sign, inner_len))
    return (result[0].reshape(length, trailing), result[1].reshape(length, trailing))


def paired_one(member, devices):
    row_count = member.shape[0]
    length = member.shape[1]
    half_len = length // 2
    slot_half = half_len // devices
    lower_half = member[:, :half_len].reshape(row_count, devices, slot_half)
    upper_half = jnp.flip(member[:, half_len:], axis=1).reshape(row_count, devices, slot_half)
    return jnp.concatenate([lower_half, upper_half], axis=2).reshape(row_count, length)


def unpaired_one(member, devices):
    row_count = member.shape[0]
    length = member.shape[1]
    half_len = length // 2
    slot_half = half_len // devices
    shaped = member.reshape(row_count, devices, 2 * slot_half)
    lower_half = shaped[:, :, :slot_half].reshape(row_count, half_len)
    upper_half = jnp.flip(shaped[:, :, slot_half:].reshape(row_count, half_len), axis=1)
    return jnp.concatenate([lower_half, upper_half], axis=1)


def to_paired(values, devices):
    return (paired_one(values[0], devices), paired_one(values[1], devices))


def from_paired(values, devices):
    return (unpaired_one(values[0], devices), unpaired_one(values[1], devices))


def to_columns(values):
    return (
        lax.all_to_all(values[0], ("fft", "grp"), split_axis=1, concat_axis=0, tiled=True),
        lax.all_to_all(values[1], ("fft", "grp"), split_axis=1, concat_axis=0, tiled=True),
    )


def to_rows(values):
    return (
        lax.all_to_all(values[0], ("fft", "grp"), split_axis=0, concat_axis=1, tiled=True),
        lax.all_to_all(values[1], ("fft", "grp"), split_axis=0, concat_axis=1, tiled=True),
    )


def negated_bins(spectrum):
    slots = spectrum[0].shape[1]
    slot_half = slots // 2
    device_index = lax.axis_index(("fft", "grp"))
    last_device = lax.axis_size(("fft", "grp")) - 1
    stacked = jnp.stack([spectrum[0], spectrum[1]])
    padded = padded_2(stacked, ((("fft", "grp"), 2),), 1)
    slot_ids = lax.broadcasted_iota(jnp.int32, (slots,), 0)
    left_pick = jnp.where(device_index == 0, 1, 0)
    right_pick = jnp.where(device_index == last_device, slots, slots + 1)
    middle_pick = jnp.where(slot_ids < slot_half, slot_half + slot_ids, slot_ids - slot_half + 2)
    picked = jnp.where(
        slot_ids == 0, left_pick, jnp.where(slot_ids == slots - 1, right_pick, middle_pick)
    )
    source_ids = lax.broadcasted_iota(jnp.int32, (slots + 2, slots), 0)
    select = (source_ids == picked[None, :]).astype(jnp.float32)
    source = jnp.einsum("qci,ij->qcj", padded, select, precision=HIGHEST)
    mirror = jnp.flip(source, axis=1)
    rolled = jnp.roll(mirror, 1, axis=1)
    fix_mask = jnp.logical_and(slot_ids == 0, device_index == 0)[None, None, :]
    mirror = jnp.where(fix_mask, rolled, mirror)
    return (mirror[0], mirror[1])


def on_device(limbs_a, limbs_b):
    devices = lax.axis_size(("fft", "grp"))
    first_col = lax.axis_index(("fft", "grp")) * limbs_a.shape[0]
    packed = (limbs_a.astype(jnp.float32), limbs_b.astype(jnp.float32))
    spectrum_rows = to_paired(transform_last(packed, ROWS, -1.0, first_col, True, False), devices)
    spectrum = transform_first(to_columns(spectrum_rows), COLS, -1.0)
    mirror = negated_bins(spectrum)
    first_part = ((spectrum[0] + mirror[0]) * 0.5, (spectrum[1] - mirror[1]) * 0.5)
    second_part = ((spectrum[1] + mirror[1]) * 0.5, (mirror[0] - spectrum[0]) * 0.5)
    pointwise = complex_times(first_part, second_part)
    coeff_rows = from_paired(to_rows(transform_first(pointwise, COLS, 1.0)), devices)
    result = transform_last(coeff_rows, ROWS, 1.0, first_col, False, True)
    total = ROWS * COLS
    out_scale = 1.0 / (total * DIGIT_VAR * math.sqrt(total // 2))
    return result * out_scale


def solution(mesh):
    placed = (P(("fft", "grp"), None), P(("fft", "grp"), None))
    return jax.shard_map(
        on_device, mesh=mesh, in_specs=placed, out_specs=P(("fft", "grp"), None), check_vma=False
    )
```

profile of v0, /device:TPU:0, one launch (start us, length us, event | category | flops | bytes accessed | tf_op | source)
XLA Modules:
  0.0 1943.9 jit_solution(9514394965965020619)
XLA Ops:
  3.3 31.9 %fusion.132 = f32[128,128,128]{2,1,0:T(8,128)S(1)} fusion(f32[128,64,128]{2,1,0:T(8,128)S(1)} %bitcast.116, s32[128]{0:T(128)S(1)} %iota_add_fusion.2), kind=kOutput, calls=%fused_computation.158 | convolution fusion | flops 1651507200 | bytes 12583424 | tf_op jit(solution)/shard_map/phl,phk->pkl/dot_general | solution.py:58
  35.2 33.0 %fusion.138 = f32[128,128,128]{2,1,0:T(8,128)} fusion(f32[128,64,128]{2,1,0:T(8,128)S(1)} %bitcast.117, s32[128]{0:T(128)S(1)} %iota_add_fusion.2), kind=kOutput, calls=%fused_computation.161 | convolution fusion | flops 1651507200 | bytes 12583424 | tf_op jit(solution)/shard_map/phl,phk->pkl/dot_general | solution.py:55
  69.5 32.7 %fusion.134 = f32[128,128,128]{2,1,0:T(8,128)} fusion(f32[128,64,128]{2,1,0:T(8,128)S(1)} %bitcast.114, s32[128]{0:T(128)S(1)} %iota_add_fusion.2), kind=kOutput, calls=%fused_computation.159 | convolution fusion | flops 1651507200 | bytes 12583424 | tf_op jit(solution)/shard_map/phl,phk->pkl/dot_general | solution.py:55
  102.3 33.9 %multiply_add_fusion.3 = (f32[128,128,128]{2,1,0:T(8,128)S(1)}, f32[128,128,128]{2,1,0:T(8,128)S(1)}) fusion(f32[128,128]{1,0:T(8,128)S(1)} %get-tuple-element.25, f32[128,128]{1,0:T(8,128)S(1)} %get-tuple-element.26, f32[128,128,128]{2,1,0:T(8,128)S(1)} %fusion.132, f32[128,128,128]{2,1,0:T(8,128)} %fusion.134, f32[128,128,128]{2,1,0:T(8,128)} %fusion.138, ...), kind=kOutput, calls=%fused_computation.72 | convolution fusion | flops 1668284416 | bytes 46268928 | tf_op jit(solution)/shard_map/phl,phk->pkl/dot_general | solution.py:58
  136.2 62.2 %fusion.86 = f32[128,128,128]{2,1,0:T(8,128)S(1)} fusion(f32[128,128,128]{2,1,0:T(8,128)S(1)} %get-tuple-element.5, s32[128]{0:T(128)S(1)} %iota_add_fusion.2), kind=kOutput, calls=%fused_computation.138 | convolution fusion | flops 3305111552 | bytes 16777728 | tf_op jit(solution)/shard_map/pkl,plh->phk/dot_general | solution.py:58
  198.5 56.5 %fusion.123 = f32[128,128,128]{2,1,0:T(8,128)} fusion(f32[128,128,128]{2,1,0:T(8,128)S(1)} %fusion.86, f32[128,128,128]{2,1,0:T(8,128)S(1)} %get-tuple-element.6, s32[128]{0:T(128)S(1)} %iota_add_fusion.2), kind=kOutput, calls=%fused_computation.155 | convolution fusion | flops 3307208704 | bytes 25166336 | tf_op jit(solution)/shard_map/pkl,plh->phk/dot_general | solution.py:58
  255.0 9.6 copy.72
  272.0 32.3 %rev.18 = f32[128,8192]{0,1:T(8,128)} reverse(f32[128,8192]{0,1:T(8,128)} %get-tuple-element.22), dimensions={1} | reverse | bytes 8388608 | tf_op jit(solution)/shard_map/jit(_flip)/rev | solution.py:130
  319.4 59.2 %fusion.88 = f32[128,128,128]{2,1,0:T(8,128)S(1)} fusion(f32[128,128,128]{2,1,0:T(8,128)} %copy-done.20, s32[128]{0:T(128)S(1)} %iota_add_fusion.2), kind=kOutput, calls=%fused_computation.139 | convolution fusion | flops 3305111552 | bytes 16777728 | tf_op jit(solution)/shard_map/pkl,plh->phk/dot_general | solution.py:55
  378.6 56.2 %fusion.120 = f32[128,128,128]{2,1,0:T(8,128)} fusion(f32[128,128,128]{2,1,0:T(8,128)S(1)} %fusion.88, f32[128,128,128]{2,1,0:T(8,128)} %copy-done.19, s32[128]{0:T(128)S(1)} %iota_add_fusion.2), kind=kOutput, calls=%fused_computation.154 | convolution fusion | flops 3307208704 | bytes 25166336 | tf_op jit(solution)/shard_map/pkl,plh->phk/dot_general | solution.py:55
  434.8 9.3 copy.71
  451.4 32.3 %rev.17 = f32[128,8192]{0,1:T(8,128)} reverse(f32[128,8192]{0,1:T(8,128)} %get-tuple-element.24), dimensions={1} | reverse | bytes 8388608 | tf_op jit(solution)/shard_map/jit(_flip)/rev | solution.py:130
  491.4 14.1 all-to-all-done.1
  520.0 17.8 fusion.57
  537.8 13.7 fusion.59
  551.5 144.7 %all-to-all-done = f32[128,32,512]{0,2,1:T(8,128)} async-done(((f32[128,32,512]{0,2,1:T(8,128)}), f32[128,32,512]{0,2,1:T(8,128)}, u32[]{:S(2)}, u32[]{:S(2)}) %all-to-all-start) | async-done | bytes 8388640 | tf_op jit(solution)/shard_map/all_to_all | solution.py:155
  696.2 8.9 copy.37
  705.2 17.7 fusion.63
  722.8 24.5 %multiply_subtract_fusion.2 = (f32[64,64,512]{2,0,1:T(8,128)}, f32[64,64,512]{2,0,1:T(8,128)}) fusion(f32[64,64]{0,1:T(8,128)S(1)} %get-tuple-element.27, f32[64,64]{0,1:T(8,128)S(1)} %get-tuple-element.28, f32[64,64,512]{2,0,1:T(8,128)} %fusion.57, f32[64,64,512]{2,0,1:T(8,128)} %fusion.63, f32[64,64,512]{2,0,1:T(8,128)} %fusion.59, ...), kind=kOutput, calls=%fused_computation.71 | convolution fusion | flops 1627447296 | bytes 50364416 | tf_op jit(solution)/shard_map/hlq,hk->klq/dot_general | solution.py:58
  747.4 16.8 fusion.49
  764.2 13.3 fusion.51
  777.5 12.0 fusion.111
  797.9 9.0 copy.52
  806.9 18.7 fusion.108
  851.3 24.1 %fusion = f32[2,4096,512]{2,1,0:T(8,128)S(1)} fusion(f32[2,4096,1]{1,2,0:T(1,128)S(1)} %collective-permute-done.1, f32[1,4096,512]{1,2,0:T(8,128)} %copy.52, f32[1,4096,512]{1,2,0:T(8,128)S(1)} %copy-done.7, f32[2,4096,1]{1,2,0:T(1,128)S(1)} %collective-permute-done, s32[512]{0:T(512)S(1)} %fusion.211), kind=kOutput, calls=%fused_computation | convolution fusion | flops 25883361280 | bytes 33622016 | tf_op jit(solution)/shard_map/qci,ij->qcj/dot_general | solution.py:183
  887.8 127.6 %rev.19 = f32[2,4096,512]{2,1,0:T(8,128)} reverse(f32[2,4096,512]{2,1,0:T(8,128)} %copy-done.6), dimensions={1} | reverse | bytes 33554432 | tf_op jit(solution)/shard_map/jit(_flip)/rev | solution.py:184
  1016.2 132.0 %slice.56 = f32[2,4095,512]{2,1,0:T(8,128)} reverse(f32[2,4095,512]{2,1,0:T(8,128)} %slice.68), dimensions={1} | reverse | bytes 33546240 | tf_op jit(solution)/shard_map/jit(_roll_static)/slice | solution.py:185
  1148.1 11.7 maximum_select_fusion
  1166.6 24.6 %multiply_add_fusion.1 = (f32[64,64,512]{2,0,1:T(8,128)}, f32[64,64,512]{2,0,1:T(8,128)}) fusion(f32[64,64,512]{2,0,1:T(8,128)} %copy-done.2, f32[64,64,512]{2,1,0:T(8,128)} %bitcast.104, f32[64,64,512]{2,0,1:T(8,128)} %copy-done.1, f32[64,64,512]{2,1,0:T(8,128)} %bitcast.103), kind=kLoop, calls=%fused_computation.64 | loop fusion | flops 29360128 | bytes 50331648 | tf_op jit(solution)/shard_map/add | solution.py:66
  1191.1 12.1 fusion.154
  1203.3 10.3 fusion.166
  1213.5 9.9 fusion.168
  1223.5 19.2 multiply_subtract_fusion
  1242.7 16.7 fusion.41
  1259.4 12.0 fusion.117
  1285.4 16.3 fusion.43
  1301.7 17.1 fusion.114
  1327.0 143.7 %all-to-all-done.3 = f32[32,128,512]{2,1,0:T(8,128)} async-done(((f32[32,128,512]{2,1,0:T(8,128)}), f32[32,128,512]{2,1,0:T(8,128)}, u32[]{:S(2)}, u32[]{:S(2)}) %all-to-all-start.3) | async-done | bytes 8388640 | tf_op jit(solution)/shard_map/all_to_all | solution.py:163
  1490.6 32.3 %rev.21 = f32[128,8192]{0,1:T(8,128)} reverse(f32[128,8192]{0,1:T(8,128)} %bitcast.105), dimensions={1} | reverse | bytes 8388608 | tf_op jit(solution)/shard_map/jit(_flip)/rev | solution.py:141
  1539.8 45.5 %fusion.66 = f32[128,128,128]{2,1,0:T(8,128)} fusion(f32[128,64,128]{2,1,0:T(8,128)} %copy.70, f32[128,64,128]{2,1,0:T(8,128)} %concatenate.36, s32[128]{0:T(128)S(1)} %copy-done.18), kind=kOutput, calls=%fused_computation.107 | convolution fusion | flops 3307208704 | bytes 16777728 | tf_op jit(solution)/shard_map/phl,phk->pkl/dot_general | solution.py:55
  1585.3 48.0 %fusion.65 = f32[128,128,128]{2,1,0:T(8,128)} fusion(f32[128,64,128]{2,1,0:T(8,128)S(1)} %copy-done.9, f32[128,64,128]{2,1,0:T(8,128)S(1)} %copy-done.11, s32[128]{0:T(128)S(1)} %copy-done.18), kind=kOutput, calls=%fused_computation.106 | convolution fusion | flops 3307208704 | bytes 16777728 | tf_op jit(solution)/shard_map/phl,phk->pkl/dot_general | solution.py:58
  1633.2 29.1 %all-to-all-done.2 = f32[32,128,512]{2,1,0:T(8,128)} async-done(((f32[32,128,512]{2,1,0:T(8,128)}), f32[32,128,512]{2,1,0:T(8,128)}, u32[]{:S(2)}, u32[]{:S(2)}) %all-to-all-start.2) | async-done | bytes 8388640 | tf_op jit(solution)/shard_map/all_to_all | solution.py:162
  1675.8 32.3 %rev.20 = f32[128,8192]{0,1:T(8,128)} reverse(f32[128,8192]{0,1:T(8,128)} %bitcast.107), dimensions={1} | reverse | bytes 8388608 | tf_op jit(solution)/shard_map/jit(_flip)/rev | solution.py:141
  1725.0 49.6 %fusion.68 = f32[128,128,128]{2,1,0:T(8,128)S(1)} fusion(f32[128,64,128]{2,1,0:T(8,128)} %copy.69, f32[128,64,128]{2,1,0:T(8,128)} %concatenate.33, s32[128]{0:T(128)S(1)} %copy-done.18), kind=kOutput, calls=%fused_computation.109 | convolution fusion | flops 3307208704 | bytes 16777728 | tf_op jit(solution)/shard_map/phl,phk->pkl/dot_general | solution.py:55
  1774.7 55.5 %fusion.67 = f32[128,128,128]{2,1,0:T(8,128)S(1)} fusion(f32[128,64,128]{2,1,0:T(8,128)S(1)} %copy-done.10, f32[128,64,128]{2,1,0:T(8,128)S(1)} %copy-done.12, s32[128]{0:T(128)S(1)} %copy-done.18), kind=kOutput, calls=%fused_computation.108 | convolution fusion | flops 3307208704 | bytes 16777728 | tf_op jit(solution)/shard_map/phl,phk->pkl/dot_general | solution.py:58
  1833.5 49.7 %fusion.25 = f32[128,128,128]{2,1,0:T(8,128)} fusion(f32[128,128]{1,0:T(8,128)S(1)} %copy-done.15, f32[128,128]{1,0:T(8,128)S(1)} %copy-done.16, s32[128]{0:T(128)S(1)} %copy-done.18, f32[128,128,128]{2,1,0:T(8,128)S(1)} %fusion.67, f32[128,128,128]{2,1,0:T(8,128)S(1)} %bitcast.121, f32[128,128,128]{2,1,0:T(8,128)S(1)} %fusion.68, ...), kind=kOutput, calls=%fused_computation.53 | convolution fusion | flops 3313500160 | bytes 42074624 | tf_op jit(solution)/shard_map/pkl,plh->phk/dot_general | solution.py:104
  1883.2 50.5 %subtract_multiply_fusion = f32[128,128,128]{2,1,0:T(8,128)S(1)} fusion(f32[128,128,128]{2,1,0:T(8,128)} %fusion.25, f32[128,128]{1,0:T(8,128)S(1)} %copy-done.15, f32[128,128]{1,0:T(8,128)S(1)} %copy-done.16, f32[128,128,128]{2,1,0:T(8,128)} %copy-done.21, f32[128,128,128]{2,1,0:T(8,128)S(1)} %bitcast.121, f32[128,128,128]{2,1,0:T(8,128)S(1)} %fusion.68, ...), kind=kOutput, calls=%fused_computation.52 | convolution fusion | flops 3317694464 | bytes 50463232 | tf_op jit(solution)/shard_map/pkl,plh->phk/dot_general | solution.py:102
  1933.7 9.9 copy.131
  (107 shorter events, 203.4 us)
Async XLA Ops:
  0.0 378.6 %copy-start.17 = (s32[128]{0:T(128)}, s32[128]{0:T(128)S(1)}, u32[]{:S(2)}) copy-start(s32[128]{0:T(128)S(1)} %iota_add_fusion.2) | copy-start | bytes 1540
  35.2 33.3 %copy-start.8 = (s32[128,8192]{1,0:T(8,128)S(1)}, s32[128,8192]{1,0:T(8,128)}, u32[]{:S(2)}) copy-start(s32[128,8192]{1,0:T(8,128)} %param.2) | copy-start | bytes 12582916
  136.2 62.2 %copy-start.19 = (f32[128,128,128]{2,1,0:T(8,128)}, f32[128,128,128]{2,1,0:T(8,128)S(1)}, u32[]{:S(2)}) copy-start(f32[128,128,128]{2,1,0:T(8,128)S(1)} %get-tuple-element.5) | copy-start | bytes 25165828
  136.2 62.2 %copy-start.20 = (f32[128,128,128]{2,1,0:T(8,128)}, f32[128,128,128]{2,1,0:T(8,128)S(1)}, u32[]{:S(2)}) copy-start(f32[128,128,128]{2,1,0:T(8,128)S(1)} %get-tuple-element.6) | copy-start | bytes 25165828
  312.0 193.5 %all-to-all-start.1 = ((f32[128,32,512]{0,2,1:T(8,128)}), f32[128,32,512]{0,2,1:T(8,128)}, u32[]{:S(2)}, u32[]{:S(2)}) async-start(f32[128,32,512]{0,2,1:T(8,128)} %pad_maximum_fusion.1), calls=%async_computation.1 | async-start | bytes 16777216 | tf_op jit(solution)/shard_map/all_to_all | solution.py:156
  505.5 190.7 %all-to-all-start = ((f32[128,32,512]{0,2,1:T(8,128)}), f32[128,32,512]{0,2,1:T(8,128)}, u32[]{:S(2)}, u32[]{:S(2)}) async-start(f32[128,32,512]{0,2,1:T(8,128)} %pad_maximum_fusion), calls=%async_computation | async-start | bytes 16777216 | tf_op jit(solution)/shard_map/all_to_all | solution.py:155
  520.0 17.8 copy-start.3
  747.4 16.8 copy-start.4
  747.4 30.1 %slice-start = ((s8[8388608]{0:T(1024)(128)(4,1)}), s8[4194304]{0:T(1024)(128)(4,1)S(1)}, s32[]{:S(2)}) async-start(s8[8388608]{0:T(1024)(128)(4,1)} %bitcast.89), calls=%async_computation.4 | async-start | bytes 8388608
  764.2 13.3 slice-start.1
  789.5 8.4 copy-start.1
  825.5 8.2 copy-start.2
  842.6 8.7 copy-start.7
  843.9 3.1 collective-permute-start
  845.5 5.8 collective-permute-start.1
  875.4 5.8 copy-start.6
  1191.1 12.1 copy-start.5
  1191.1 22.4 %slice-start.2 = ((s8[8388608]{0:T(1024)(128)(4,1)}), s8[4194304]{0:T(1024)(128)(4,1)S(1)}, s32[]{:S(2)}) async-start(s8[8388608]{0:T(1024)(128)(4,1)} %bitcast.95), calls=%async_computation.6 | async-start | bytes 8388608
  1203.3 10.3 slice-start.3
  1213.5 10.0 copy-start.13
  1213.5 10.0 copy-start.14
  1242.7 16.8 copy-start
  1279.8 191.0 %all-to-all-start.3 = ((f32[32,128,512]{2,1,0:T(8,128)}), f32[32,128,512]{2,1,0:T(8,128)}, u32[]{:S(2)}, u32[]{:S(2)}) async-start(f32[32,128,512]{2,1,0:T(8,128)} %bitcast.98), calls=%async_computation.3 | async-start | bytes 16777216 | tf_op jit(solution)/shard_map/all_to_all | solution.py:163
  1470.7 191.6 %all-to-all-start.2 = ((f32[32,128,512]{2,1,0:T(8,128)}), f32[32,128,512]{2,1,0:T(8,128)}, u32[]{:S(2)}, u32[]{:S(2)}) async-start(f32[32,128,512]{2,1,0:T(8,128)} %bitcast.97), calls=%async_computation.2 | async-start | bytes 16777216 | tf_op jit(solution)/shard_map/all_to_all | solution.py:162
  1528.3 11.5 copy-start.18
  1539.7 45.5 %copy-start.9 = (f32[128,64,128]{2,1,0:T(8,128)S(1)}, f32[128,64,128]{2,1,0:T(8,128)}, u32[]{:S(2)}) copy-start(f32[128,64,128]{2,1,0:T(8,128)} %copy.70) | copy-start | bytes 12582916
  1539.7 45.5 %copy-start.11 = (f32[128,64,128]{2,1,0:T(8,128)S(1)}, f32[128,64,128]{2,1,0:T(8,128)}, u32[]{:S(2)}) copy-start(f32[128,64,128]{2,1,0:T(8,128)} %concatenate.36) | copy-start | bytes 12582916
  1725.0 49.7 %copy-start.10 = (f32[128,64,128]{2,1,0:T(8,128)S(1)}, f32[128,64,128]{2,1,0:T(8,128)}, u32[]{:S(2)}) copy-start(f32[128,64,128]{2,1,0:T(8,128)} %copy.69) | copy-start | bytes 12582916
  1725.0 49.7 %copy-start.12 = (f32[128,64,128]{2,1,0:T(8,128)S(1)}, f32[128,64,128]{2,1,0:T(8,128)}, u32[]{:S(2)}) copy-start(f32[128,64,128]{2,1,0:T(8,128)} %concatenate.33) | copy-start | bytes 12582916
  1725.0 108.5 %slice-start.4 = ((s8[8388608]{0:T(1024)(128)(4,1)}), s8[4194304]{0:T(1024)(128)(4,1)S(1)}, s32[]{:S(2)}) async-start(s8[8388608]{0:T(1024)(128)(4,1)} %bitcast.118), calls=%async_computation.8 | async-start | bytes 8388608
  1725.0 108.5 %slice-start.6 = ((s8[8388608]{0:T(1024)(128)(4,1)}), s8[4194304]{0:T(1024)(128)(4,1)S(1)}, s32[]{:S(2)}) async-start(s8[8388608]{0:T(1024)(128)(4,1)} %bitcast.120), calls=%async_computation.10 | async-start | bytes 8388608
  1774.6 58.9 %copy-start.15 = (f32[128,128]{1,0:T(8,128)S(1)}, f32[128,128]{1,0:T(8,128)}, u32[]{:S(2)}) copy-start(f32[128,128]{1,0:T(8,128)} %get-tuple-element.31) | copy-start | bytes 196612
  1774.6 58.9 %copy-start.16 = (f32[128,128]{1,0:T(8,128)S(1)}, f32[128,128]{1,0:T(8,128)}, u32[]{:S(2)}) copy-start(f32[128,128]{1,0:T(8,128)} %get-tuple-element.32) | copy-start | bytes 196612
  1774.7 58.9 %slice-start.5 = ((s8[8388608]{0:T(1024)(128)(4,1)}), s8[4194304]{0:T(1024)(128)(4,1)S(1)}, s32[]{:S(2)}) async-start(s8[8388608]{0:T(1024)(128)(4,1)} %bitcast.118), calls=%async_computation.9 | async-start | bytes 8388608
  1774.7 58.9 %slice-start.7 = ((s8[8388608]{0:T(1024)(128)(4,1)}), s8[4194304]{0:T(1024)(128)(4,1)S(1)}, s32[]{:S(2)}) async-start(s8[8388608]{0:T(1024)(128)(4,1)} %bitcast.120), calls=%async_computation.11 | async-start | bytes 8388608
  1830.2 3.3 copy-start.21
where the time goes:
time: 1980 us; the launch traced here: 1940 us
  matrix products  937 us (47%)
  local copies, waits for them, and re-layouts  586 us (30%)
  waiting for transfers between devices  336 us (17%)
  other arithmetic  58 us (3%)
  starting transfers between devices  26 us (1%)
    dot_general x7, matrix products, complex_einsum(): jnp.einsum(pattern, left_side[0], right_side[1], precision=HIGHEST)  214 us
    dot_general x7, matrix products, complex_einsum(): jnp.einsum(pattern, left_side[0], right_side[0], precision=HIGHEST)  205 us
    dot_general x7, matrix products, complex_einsum(): jnp.einsum(pattern, left_side[1], right_side[0], precision=HIGHEST)  204 us
    dot_general x7, matrix products, complex_einsum(): jnp.einsum(pattern, left_side[1], right_side[1], precision=HIGHEST)  190 us
    all_to_all x1, waiting for transfers between devices, to_columns(): lax.all_to_all(values[0], ('fft', 'grp'), split_axis=1, concat_axis=0, ti...  145 us
    all_to_all x1, waiting for transfers between devices, to_rows(): lax.all_to_all(values[1], ('fft', 'grp'), split_axis=0, concat_axis=1, ti...  144 us
    slice x3, local copies, waits for them, and re-layouts, negated_bins(): rolled = jnp.roll(mirror, 1, axis=1)  139 us
    rev x1, local copies, waits for them, and re-layouts, negated_bins(): mirror = jnp.flip(source, axis=1)  128 us
  transfers between devices with their start and end apart: 6, of which 6 were waited for; matrix products, arithmetic and copies ran while one was open for 21% of the time, Pallas kernels for 0%

commit v1 on v0

v1 whole, which is shorter than its diff:
```python
import functools
import math

import jax
import jax.numpy as jnp
import numpy as np
from jax import lax
from jax.experimental import pallas as pl
from jax.experimental.pallas import tpu as pltpu
from jax.sharding import PartitionSpec as P

DIGIT_VAR = 5461.25
INNER = 128
AXES = ("fft", "grp")
BF16 = jnp.bfloat16
F32 = jnp.float32


def split(value):
    high = value.astype(BF16)
    return (high, (value - high.astype(F32)).astype(BF16))


def three_dot(left, right, dims):
    def one(x, y):
        return lax.dot_general(x, y, (dims, ((), ())), preferred_element_type=F32)

    return one(left[0], right[0]) + (one(left[1], right[0]) + one(left[0], right[1]))


def rotate(re, im, turn):
    num, den = turn
    num = num % den
    if num == 0:
        return (re, im)
    if 4 * num == den:
        return (-im, re)
    if 2 * num == den:
        return (-re, -im)
    if 4 * num == 3 * den:
        return (im, -re)
    angle = 2.0 * math.pi * num / den
    cos, sin = (math.cos(angle), math.sin(angle))
    return (re * cos - im * sin, re * sin + im * cos)


def fft_list(values, sign):
    size = len(values)
    if size == 1:
        return values
    even = fft_list(values[0::2], sign)
    odd = fft_list(values[1::2], sign)
    low, high = ([], [])
    for k in range(size // 2):
        (er, ei), (r, i) = (even[k], odd[k])
        if 8 * k == size or 8 * k == 3 * size:
            root = math.sqrt(0.5)
            if 8 * k == size:
                tr, ti = ((r - sign * i) * root, (i + sign * r) * root)
            else:
                tr, ti = ((-r - sign * i) * root, (sign * r - i) * root)
            low.append((er + tr, ei + ti))
            high.append((er - tr, ei - ti))
        elif 4 * k == size:
            if sign > 0:
                low.append((er - i, ei + r))
                high.append((er + i, ei - r))
            else:
                low.append((er + i, ei - r))
                high.append((er - i, ei + r))
        else:
            tr, ti = rotate(r, i, (sign * k, size))
            low.append((er + tr, ei + ti))
            high.append((er - tr, ei - ti))
    return low + high


def times(x, y):
    return (x[0] * y[0] - x[1] * y[1], x[0] * y[1] + x[1] * y[0])


def times_conj(x, y):
    return (x[0] * y[0] + x[1] * y[1], x[1] * y[0] - x[0] * y[1])


def first_kernel(outer, a_ref, b_ref, cos_ref, sin_ref, sa_ref, sb_ref):
    for src, dst in ((a_ref, sa_ref), (b_ref, sb_ref)):
        terms = []
        for r in range(outer):
            digit = src[:, r * INNER : (r + 1) * INNER].astype(F32)
            angle = -2.0 * math.pi * r / (4 * outer)
            if r == 0:
                terms.append((digit, jnp.zeros_like(digit)))
            else:
                terms.append((digit * math.cos(angle), digit * math.sin(angle)))
        result = fft_list(terms, -1)
        for j in range(outer):
            re, im = times_conj(result[j], (cos_ref[j : j + 1, :], sin_ref[j : j + 1, :]))
            dst[j, :, :INNER] = re
            dst[j, :, INNER:] = im


def first_stage(limbs_a, limbs_b, cos, sin):
    cols, length = limbs_a.shape
    outer = length // INNER
    rows = 8
    in_spec = pl.BlockSpec((rows, length), lambda i: (i, 0))
    table = pl.BlockSpec((outer, INNER), lambda i: (0, 0))
    out_spec = pl.BlockSpec((outer, rows, 2 * INNER), lambda i: (0, i, 0))
    out = jax.ShapeDtypeStruct((outer, cols, 2 * INNER), F32)
    return pl.pallas_call(
        functools.partial(first_kernel, outer),
        grid=(cols // rows,),
        in_specs=[in_spec, in_spec, table, table],
        out_specs=[out_spec, out_spec],
        out_shape=[out, out],
        cost_estimate=pl.CostEstimate(
            flops=100 * cols * length, bytes_accessed=24 * cols * length, transcendentals=0
        ),
        name="first_stage",
    )(limbs_a, limbs_b, cos, sin)


def second_kernel(group, sa_ref, sb_ref, table_ref, out_ref, high_ref, low_ref):
    @pl.when(pl.program_id(0) == 0)
    def _():
        high_ref[...], low_ref[...] = split(table_ref[...])

    cols = sa_ref.shape[2]
    table = (high_ref[...], low_ref[...])
    for g in range(group):
        for at, src in ((0, sa_ref), (2, sb_ref)):
            result = three_dot(table, split(src[g, 0]), ((1,), (1,)))
            out_ref[g, at] = result[:INNER]
            out_ref[g, at + 1] = result[INNER:]


def second_stage(sa, sb, table, chunk, chunks):
    outer, cols, width = sa.shape
    count = outer // chunks
    group = 2 if count % 2 == 0 else 1
    shaped = (count, chunks, cols, width)
    spec = pl.BlockSpec((group, 1, cols, width), lambda i: (i, chunk, 0, 0))
    return pl.pallas_call(
        functools.partial(second_kernel, group),
        grid=(count // group,),
        in_specs=[spec, spec, pl.BlockSpec((width, width), lambda i: (0, 0))],
        out_specs=pl.BlockSpec((group, 4, INNER, cols), lambda i: (i, 0, 0, 0)),
        out_shape=jax.ShapeDtypeStruct((count, 4, INNER, cols), F32),
        scratch_shapes=[pltpu.VMEM((width, width), BF16)] * 2,
        cost_estimate=pl.CostEstimate(
            flops=12 * count * cols * width * width, bytes_accessed=16 * count * cols * width, transcendentals=0
        ),
        name="second_stage",
    )(sa.reshape(shaped), sb.reshape(shaped), table)


def middle_kernel(devices, x_ref, ka_cos, ka_sin, q_cos, q_sin, fh, fl, ih, il, v_ref, ya, yb):
    cols = x_ref.shape[3]
    rows = x_ref.shape[2]
    q_turn = (q_cos[...], q_sin[...])

    def turn_of(k):
        return times((ka_cos[k : k + 1, :], ka_sin[k : k + 1, :]), q_turn)

    for at, dst in ((0, ya), (2, yb)):
        result = fft_list([(x_ref[d, at], x_ref[d, at + 1]) for d in range(devices)], -1)
        for k in range(devices):
            re, im = times_conj(result[k], turn_of(k))
            dst[k * rows : (k + 1) * rows, :cols] = re
            dst[k * rows : (k + 1) * rows, cols:] = im
    forward = (fh[...], fl[...])
    inverse = (ih[...], il[...])
    a = three_dot(split(ya[...]), forward, ((1,), (0,)))
    b = three_dot(split(yb[...]), forward, ((1,), (0,)))
    re, im = times((a[:, :cols], a[:, cols:]), (b[:, :cols], b[:, cols:]))
    ya[:, :cols] = re
    ya[:, cols:] = im
    yb[...] = three_dot(split(ya[...]), inverse, ((1,), (0,)))
    terms = []
    for k in range(devices):
        part = slice(k * rows, (k + 1) * rows)
        terms.append(times((yb[part, :cols], yb[part, cols:]), turn_of(k)))
    result = fft_list(terms, 1)
    for d in range(devices):
        v_ref[d, 0] = result[d][0]
        v_ref[d, 1] = result[d][1]


def middle_stage(x, ka_cos, ka_sin, q_cos, q_sin, tables):
    devices, _, count, cols = x.shape
    rows = 8
    whole = lambda t: pl.BlockSpec(t.shape, lambda i: (0, 0))
    q_spec = pl.BlockSpec((rows, cols), lambda i: (i, 0))
    return pl.pallas_call(
        functools.partial(middle_kernel, devices),
        grid=(count // rows,),
        in_specs=[
            pl.BlockSpec((devices, 4, rows, cols), lambda i: (0, 0, i, 0)),
            whole(ka_cos),
            whole(ka_sin),
            q_spec,
            q_spec,
        ]
        + [whole(t) for t in tables],
        out_specs=pl.BlockSpec((devices, 2, rows, cols), lambda i: (0, 0, i, 0)),
        out_shape=jax.ShapeDtypeStruct((devices, 2, count, cols), F32),
        scratch_shapes=[pltpu.VMEM((devices * rows, 2 * cols), F32)] * 2,
        cost_estimate=pl.CostEstimate(
            flops=36 * devices * count * cols * cols * 4, bytes_accessed=24 * devices * count * cols, transcendentals=0
        ),
        name="middle_stage",
    )(x, ka_cos, ka_sin, q_cos, q_sin, *tables)


def third_kernel(group, v_ref, table_ref, cos_ref, sin_ref, g_ref, high_ref, low_ref):
    @pl.when(pl.program_id(0) == 0)
    def _():
        high_ref[...], low_ref[...] = split(table_ref[...])

    table = (high_ref[...], low_ref[...])
    for g in range(group):
        stacked = jnp.concatenate([v_ref[g, 0].T, v_ref[g, 1].T], axis=1)
        result = three_dot(split(stacked), table, ((1,), (0,)))
        turn = (cos_ref[g], sin_ref[g])
        re, im = times((result[:, :INNER], result[:, INNER:]), turn)
        g_ref[g, :, :INNER] = re
        g_ref[g, :, INNER:] = im


def third_stage(v, table, cos, sin, chunk, chunks):
    count, _, _, cols = v.shape
    group = 2 if count % 2 == 0 else 1
    width = 2 * INNER
    turns = pl.BlockSpec((group, 1, INNER), lambda i: (i, 0, 0))
    cos = cos.reshape(count, chunks, INNER)[:, chunk][:, None]
    sin = sin.reshape(count, chunks, INNER)[:, chunk][:, None]
    return pl.pallas_call(
        functools.partial(third_kernel, group),
        grid=(count // group,),
        in_specs=[
            pl.BlockSpec((group, 2, INNER, cols), lambda i: (i, 0, 0, 0)),
            pl.BlockSpec((width, width), lambda i: (0, 0)),
            turns,
            turns,
        ],
        out_specs=pl.BlockSpec((group, cols, width), lambda i: (i, 0, 0)),
        out_shape=jax.ShapeDtypeStruct((count, cols, width), F32),
        scratch_shapes=[pltpu.VMEM((width, width), BF16)] * 2,
        cost_estimate=pl.CostEstimate(
            flops=6 * count * cols * width * width, bytes_accessed=8 * count * cols * width, transcendentals=0
        ),
        name="third_stage",
    )(v, table, cos, sin)


def last_kernel(outer, scale, *refs):
    out_ref = refs[-1]
    chunks = len(refs) - 1
    terms = []
    for j in range(outer):
        src = refs[j % chunks]
        terms.append((src[j // chunks, :, :INNER], src[j // chunks, :, INNER:]))
    result = fft_list(terms, 1)
    for r in range(outer):
        angle = 2.0 * math.pi * r / (4 * outer)
        cos, sin = (math.cos(angle) * scale, math.sin(angle) * scale)
        re, im = result[r]
        at = r * INNER
        out_ref[:, at : at + INNER] = re * cos - im * sin
        at = at + outer * INNER
        out_ref[:, at : at + INNER] = -(re * sin + im * cos)


def last_stage(parts, scale):
    chunks = len(parts)
    count, cols, width = parts[0].shape
    outer = count * chunks
    rows = 8
    length = outer * INNER
    return pl.pallas_call(
        functools.partial(last_kernel, outer, scale),
        grid=(cols // rows,),
        in_specs=[pl.BlockSpec((count, rows, width), lambda i: (0, i, 0))] * chunks,
        out_specs=pl.BlockSpec((rows, 2 * length), lambda i: (i, 0)),
        out_shape=jax.ShapeDtypeStruct((cols, 2 * length), F32),
        cost_estimate=pl.CostEstimate(
            flops=100 * cols * length, bytes_accessed=16 * cols * length, transcendentals=0
        ),
        name="last_stage",
    )(*parts)


def turns(phase, modulus):
    angle = (phase % modulus).astype(F32) * (2.0 * math.pi / modulus)
    return (jnp.cos(angle), jnp.sin(angle))


def iota(shape, dim):
    return lax.broadcasted_iota(jnp.int32, shape, dim)


def row_turns(outer, devices, device):
    shape = (outer, INNER)
    phase = (4 * iota(shape, 0) + 1) * (devices * iota(shape, 1) + device)
    return turns(phase, 4 * outer * INNER * devices)


def row_table(devices, device):
    shape = (2 * INNER, 2 * INNER)
    row, col = (iota(shape, 0), iota(shape, 1))
    modulus = 4 * INNER * devices
    phase = 4 * (row % INNER) * (devices * (col % INNER) + device)
    quarter = INNER * devices * (row // INNER - col // INNER)
    angle = ((phase + quarter) % modulus).astype(F32) * (2.0 * math.pi / modulus)
    return jnp.cos(angle)


def spectral_turns(local, cols, devices, device, outer, total):
    shape = (local, cols)
    at = iota(shape, 0) + device * local
    freq = at // INNER + outer * (at % INNER)
    return turns(iota(shape, 1) * (4 * freq + 1), total)


def np_split(value):
    high = value.astype(np.float32).astype(BF16)
    low = (value - high.astype(np.float64)).astype(np.float32).astype(BF16)
    return (high, low)


def column_tables(cols, devices):
    k = np.arange(devices)[:, None] * np.arange(cols)[None, :]
    angle = 2.0 * np.pi * k / (cols * devices)
    n = np.arange(cols)
    theta = 2.0 * np.pi * (n[:, None] * n[None, :] % cols) / cols
    forward = np.block([[np.cos(theta), -np.sin(theta)], [np.sin(theta), np.cos(theta)]])
    tables = np_split(forward) + np_split(forward.T)
    return (np.cos(angle).astype(np.float32), np.sin(angle).astype(np.float32), tables)


def exchange(value):
    return lax.all_to_all(value, AXES, split_axis=0, concat_axis=0, tiled=True)


def on_device(limbs_a, limbs_b):
    devices = lax.axis_size(AXES)
    device = lax.axis_index(AXES)
    cols, length = limbs_a.shape
    outer = length // INNER
    total = length * cols * devices
    scale = 1.0 / (total * DIGIT_VAR * math.sqrt(total))
    chunks = max(1, outer // devices)
    pieces = max(1, devices // outer)
    local = length // devices
    cos, sin = row_turns(outer, devices, device)
    table = row_table(devices, device)
    ka_cos, ka_sin, tables = column_tables(cols, devices)
    q_cos, q_sin = spectral_turns(local, cols, devices, device, outer, 4 * total)
    each = local // chunks

    sa, sb = first_stage(limbs_a, limbs_b, cos, sin)
    arrived = []
    for h in range(chunks):
        x = second_stage(sa, sb, table, h, chunks)
        if pieces > 1:
            x = x.reshape(outer, 4, pieces, each, cols).transpose(0, 2, 1, 3, 4)
            x = x.reshape(devices, 4, each, cols)
        arrived.append(exchange(x))
    back = []
    for h in range(chunks):
        part = slice(h * each, (h + 1) * each)
        v = middle_stage(arrived[h], ka_cos, ka_sin, q_cos[part], q_sin[part], tables)
        back.append(exchange(v))
    parts = []
    for h in range(chunks):
        v = back[h]
        if pieces > 1:
            v = v.reshape(outer, pieces, 2, each, cols).transpose(0, 2, 1, 3, 4)
            v = v.reshape(outer, 2, INNER, cols)
        parts.append(third_stage(v, table, cos, sin, h, chunks))
    return last_stage(parts, scale)


def solution(mesh):
    placed = P(AXES, None)
    return jax.shard_map(
        on_device, mesh=mesh, in_specs=(placed, placed), out_specs=placed, check_vma=False
    )
```

time: 1980 us -> 644 us (0.33); the launches traced: 1940 us -> 641 us
  matrix products: 937 us -> 0 us
  local copies, waits for them, and re-layouts: 586 us -> 2.01 us
  waiting for transfers between devices: 336 us -> 491 us
  Pallas kernels: 0 us -> 125 us
  other arithmetic: 58 us -> 4.14 us
    dot_general x31 -> x0, matrix products: 937 us -> none  [the longest x7 214 us: complex_einsum(): jnp.einsum(pattern, left_side[0], right_side[1], precision=HIGHEST)]
    rev x5 -> x0, local copies, waits for them, and re-layouts: 257 us -> none  [the longest x1 128 us: negated_bins(): mirror = jnp.flip(source, axis=1)]
    slice x12 -> x3, local copies, waits for them, and re-layouts: 201 us -> 2.01 us  [the longest x1 0.68 us: on_device(): q_cos[part]]
    all_to_all x4, waiting for transfers between devices: 332 us -> 491 us  [exchange(): return lax.all_to_all(value, AXES, split_axis=0, concat_axis=0, tiled=True)]
    pallas_call x0 -> x8, Pallas kernels: none -> 125 us  [the longest x2 37 us: middle_stage(): pl.pallas_call(functools.partial(middle_kernel, devices), grid=(count //...]
    add x2 -> x4, other arithmetic: 24.6 us -> 0.02 us  [the longest x3 0.02 us: row_turns(): phase = (4 * iota(shape, 0) + 1) * (devices * iota(shape, 1) + device)]
    unnamed x63 -> x0, local copies, waits for them, and re-layouts: 20.6 us -> none
    concatenate x4 -> x0, local copies, waits for them, and re-layouts: 20.4 us -> none  [unpaired_one(): return jnp.concatenate([lower_half, upper_half], axis=1)]
  transfers between devices with their start and end apart: 6 -> 4, of which waited for: 6 -> 4; matrix products, arithmetic and copies ran while one was open for 21% -> 1% of each run, Pallas kernels for 0% -> 10%
where the time goes in v1:
time: 644 us; the launch traced here: 641 us
  waiting for transfers between devices  491 us (76%)
  Pallas kernels  125 us (19%)
  starting transfers between devices  19.9 us (3%)
    all_to_all x4, waiting for transfers between devices, exchange(): return lax.all_to_all(value, AXES, split_axis=0, concat_axis=0, tiled=True)  491 us
    pallas_call x2, Pallas kernels, middle_stage(): pl.pallas_call(functools.partial(middle_kernel, devices), grid=(count //...  37 us
    pallas_call x2, Pallas kernels, second_stage(): pl.pallas_call(functools.partial(second_kernel, group), grid=(count // gr...  32.2 us
    pallas_call x2, Pallas kernels, third_stage(): pl.pallas_call(functools.partial(third_kernel, group), grid=(count // gro...  25.6 us
    all_to_all x4, starting transfers between devices, exchange(): return lax.all_to_all(value, AXES, split_axis=0, concat_axis=0, tiled=True)  19.9 us
    pallas_call x1, Pallas kernels, first_stage(): pl.pallas_call(functools.partial(first_kernel, outer), grid=(cols // rows...  16.2 us
    pallas_call x1, Pallas kernels, last_stage(): pl.pallas_call(functools.partial(last_kernel, outer, scale), grid=(cols /...  13.6 us
  transfers between devices with their start and end apart: 4, of which 4 were waited for; matrix products, arithmetic and copies ran while one was open for 1% of the time, Pallas kernels for 10%

profile of v1, /device:TPU:0, one launch (start us, length us, event | category | flops | bytes accessed | tf_op | source)
XLA Modules:
  0.0 641.3 jit_solution(4955177417173941998)
XLA Ops:
  0.0 0.8 fusion.17
  0.9 16.2 %first_stage.1 = (f32[64,128,256]{2,1,0:T(8,128)}, f32[64,128,256]{2,1,0:T(8,128)}) custom-call(s32[128,8192]{1,0:T(8,128)} %a_ref.1, s32[128,8192]{1,0:T(8,128)} %b_ref.1, f32[64,128]{1,0:T(8,128)} %get-tuple-element.22.cos_ref, f32[64,128]{1,0:T(8,128)} %get-tuple-element.21.sin_ref), custom_call_target="tpu_custom_call" | custom-call | flops 104857600 | bytes 25165824 | tf_op jit(solution)/shard_map/first_stage/pallas_call | solution.py:111
  17.1 2.0 fusion.3.table_ref
  19.1 16.1 %second_stage.2 = f32[32,4,128,128]{3,2,1,0:T(8,128)} custom-call(f32[32,2,128,256]{3,2,1,0:T(8,128)} %bitcast.2, f32[32,2,128,256]{3,2,1,0:T(8,128)} %bitcast.4, f32[256,256]{1,0:T(8,128)} %fusion.3.table_ref), custom_call_target="tpu_custom_call" | custom-call | flops 3221225472 | bytes 16777216 | tf_op jit(solution)/shard_map/second_stage/pallas_call | solution.py:144
  35.2 7.5 %all-to-all-start = ((f32[32,4,128,128]{3,2,1,0:T(8,128)}), f32[32,4,128,128]{3,2,1,0:T(8,128)}, u32[]{:S(2)}, u32[]{:S(2)}) async-start(f32[32,4,128,128]{3,2,1,0:T(8,128)} %second_stage.2), calls=%async_computation | async-start | bytes 16777216 | tf_op jit(solution)/shard_map/all_to_all | solution.py:343
  42.6 16.1 %second_stage.3 = f32[32,4,128,128]{3,2,1,0:T(8,128)} custom-call(f32[32,2,128,256]{3,2,1,0:T(8,128)} %bitcast.3, f32[32,2,128,256]{3,2,1,0:T(8,128)} %bitcast.5, f32[256,256]{1,0:T(8,128)} %fusion.3.table_ref), custom_call_target="tpu_custom_call" | custom-call | flops 3221225472 | bytes 16777216 | tf_op jit(solution)/shard_map/second_stage/pallas_call | solution.py:144
  58.8 169.9 %all-to-all-done.x_ref = f32[32,4,128,128]{3,2,1,0:T(8,128)} async-done(((f32[32,4,128,128]{3,2,1,0:T(8,128)}), f32[32,4,128,128]{3,2,1,0:T(8,128)}, u32[]{:S(2)}, u32[]{:S(2)}) %all-to-all-start) | async-done | bytes 8388640 | tf_op jit(solution)/shard_map/all_to_all | solution.py:343
  228.7 4.4 all-to-all-start.2
  233.2 0.6 fusion.7
  233.8 0.7 fusion.23
  234.5 0.7 fusion.22
  235.2 18.5 %middle_stage.2 = f32[32,2,128,128]{3,2,1,0:T(8,128)} custom-call(f32[32,4,128,128]{3,2,1,0:T(8,128)} %all-to-all-done.x_ref, f32[32,128]{1,0:T(8,128)} %constant.146.clone.ka_cos, f32[32,128]{1,0:T(8,128)} %constant.147.clone.ka_sin, f32[128,128]{1,0:T(8,128)} %get-tuple-element.12.q_cos, f32[128,128]{1,0:T(8,128)} %get-tuple-element.10.q_sin, ...), custom_call_target="tpu_custom_call" | custom-call | flops 9663676416 | bytes 12582912 | tf_op jit(solution)/shard_map/middle_stage/pallas_call | solution.py:195
  253.6 165.6 %all-to-all-done.2.x_ref = f32[32,4,128,128]{3,2,1,0:T(8,128)} async-done(((f32[32,4,128,128]{3,2,1,0:T(8,128)}), f32[32,4,128,128]{3,2,1,0:T(8,128)}, u32[]{:S(2)}, u32[]{:S(2)}) %all-to-all-start.2) | async-done | bytes 8388640 | tf_op jit(solution)/shard_map/all_to_all | solution.py:343
  419.2 4.4 all-to-all-start.1
  423.6 18.5 %middle_stage.3 = f32[32,2,128,128]{3,2,1,0:T(8,128)} custom-call(f32[32,4,128,128]{3,2,1,0:T(8,128)} %all-to-all-done.2.x_ref, f32[32,128]{1,0:T(8,128)} %constant.146.clone.ka_cos, f32[32,128]{1,0:T(8,128)} %constant.147.clone.ka_sin, f32[128,128]{1,0:T(8,128)} %get-tuple-element.11.q_cos, f32[128,128]{1,0:T(8,128)} %get-tuple-element.9.q_sin, ...), custom_call_target="tpu_custom_call" | custom-call | flops 9663676416 | bytes 12582912 | tf_op jit(solution)/shard_map/middle_stage/pallas_call | solution.py:195
  442.1 75.3 %all-to-all-done.1.v_ref = f32[32,2,128,128]{3,2,1,0:T(8,128)} async-done(((f32[32,2,128,128]{3,2,1,0:T(8,128)}), f32[32,2,128,128]{3,2,1,0:T(8,128)}, u32[]{:S(2)}, u32[]{:S(2)}) %all-to-all-start.1) | async-done | bytes 4194336 | tf_op jit(solution)/shard_map/all_to_all | solution.py:343
  517.5 3.7 all-to-all-start.3
  521.2 0.6 fusion.15
  521.8 0.7 fusion.24
  522.4 12.8 %third_stage.2.refs_0_ = f32[32,128,256]{2,1,0:T(8,128)} custom-call(f32[32,2,128,128]{3,2,1,0:T(8,128)} %all-to-all-done.1.v_ref, f32[256,256]{1,0:T(8,128)} %fusion.3.table_ref, f32[32,1,128]{2,1,0:T(1,128)} %get-tuple-element.35.cos_ref, f32[32,1,128]{2,1,0:T(1,128)} %get-tuple-element.14.sin_ref), custom_call_target="tpu_custom_call" | custom-call | flops 1610612736 | bytes 8388608 | tf_op jit(solution)/shard_map/third_stage/pallas_call | solution.py:238
  535.2 79.8 %all-to-all-done.3.v_ref = f32[32,2,128,128]{3,2,1,0:T(8,128)} async-done(((f32[32,2,128,128]{3,2,1,0:T(8,128)}), f32[32,2,128,128]{3,2,1,0:T(8,128)}, u32[]{:S(2)}, u32[]{:S(2)}) %all-to-all-start.3) | async-done | bytes 4194336 | tf_op jit(solution)/shard_map/all_to_all | solution.py:343
  615.0 12.8 %third_stage.3.refs_1_ = f32[32,128,256]{2,1,0:T(8,128)} custom-call(f32[32,2,128,128]{3,2,1,0:T(8,128)} %all-to-all-done.3.v_ref, f32[256,256]{1,0:T(8,128)} %fusion.3.table_ref, f32[32,1,128]{2,1,0:T(1,128)} %get-tuple-element.36.cos_ref, f32[32,1,128]{2,1,0:T(1,128)} %get-tuple-element.13.sin_ref), custom_call_target="tpu_custom_call" | custom-call | flops 1610612736 | bytes 8388608 | tf_op jit(solution)/shard_map/third_stage/pallas_call | solution.py:238
  627.8 13.6 %last_stage.1 = f32[128,16384]{1,0:T(8,128)} custom-call(f32[32,128,256]{2,1,0:T(8,128)} %third_stage.2.refs_0_, f32[32,128,256]{2,1,0:T(8,128)} %third_stage.3.refs_1_), custom_call_target="tpu_custom_call" | custom-call | flops 104857600 | bytes 16777216 | tf_op jit(solution)/shard_map/last_stage/pallas_call | solution.py:281
  (9 shorter events, 0.1 us)
Async XLA Ops:
  35.2 193.5 %all-to-all-start = ((f32[32,4,128,128]{3,2,1,0:T(8,128)}), f32[32,4,128,128]{3,2,1,0:T(8,128)}, u32[]{:S(2)}, u32[]{:S(2)}) async-start(f32[32,4,128,128]{3,2,1,0:T(8,128)} %second_stage.2), calls=%async_computation | async-start | bytes 16777216 | tf_op jit(solution)/shard_map/all_to_all | solution.py:343
  228.7 190.5 %all-to-all-start.2 = ((f32[32,4,128,128]{3,2,1,0:T(8,128)}), f32[32,4,128,128]{3,2,1,0:T(8,128)}, u32[]{:S(2)}, u32[]{:S(2)}) async-start(f32[32,4,128,128]{3,2,1,0:T(8,128)} %second_stage.3), calls=%async_computation.2 | async-start | bytes 16777216 | tf_op jit(solution)/shard_map/all_to_all | solution.py:343
  419.2 98.3 %all-to-all-start.1 = ((f32[32,2,128,128]{3,2,1,0:T(8,128)}), f32[32,2,128,128]{3,2,1,0:T(8,128)}, u32[]{:S(2)}, u32[]{:S(2)}) async-start(f32[32,2,128,128]{3,2,1,0:T(8,128)} %middle_stage.2), calls=%async_computation.1 | async-start | bytes 8388608 | tf_op jit(solution)/shard_map/all_to_all | solution.py:343
  517.5 97.5 %all-to-all-start.3 = ((f32[32,2,128,128]{3,2,1,0:T(8,128)}), f32[32,2,128,128]{3,2,1,0:T(8,128)}, u32[]{:S(2)}, u32[]{:S(2)}) async-start(f32[32,2,128,128]{3,2,1,0:T(8,128)} %middle_stage.3), calls=%async_computation.3 | async-start | bytes 8388608 | tf_op jit(solution)/shard_map/all_to_all | solution.py:343

commit v2 on v1

v2 whole, which is shorter than its diff:
```python
import functools
import math

import jax
import jax.numpy as jnp
import numpy as np
from jax import lax
from jax.experimental import pallas as pl
from jax.experimental.pallas import tpu as pltpu
from jax.sharding import PartitionSpec as P

DIGIT_VAR = 5461.25
INNER = 128
ROWS_STEP = 8
AXES = ("fft", "grp")
BF16 = jnp.bfloat16
F32 = jnp.float32


def split(value):
    high = value.astype(BF16)
    return (high, (value - high.astype(F32)).astype(BF16))


def three_dot(left, right, dims):
    def one(x, y):
        return lax.dot_general(x, y, (dims, ((), ())), preferred_element_type=F32)

    return one(left[0], right[0]) + (one(left[1], right[0]) + one(left[0], right[1]))


def rotate(re, im, turn):
    num, den = turn
    num = num % den
    if num == 0:
        return (re, im)
    if 4 * num == den:
        return (-im, re)
    if 2 * num == den:
        return (-re, -im)
    if 4 * num == 3 * den:
        return (im, -re)
    if 8 * num == den:
        return ((re - im) * math.sqrt(0.5), (re + im) * math.sqrt(0.5))
    angle = 2.0 * math.pi * num / den
    cos, sin = (math.cos(angle), math.sin(angle))
    return (re * cos - im * sin, re * sin + im * cos)


def fft_list(values, sign):
    size = len(values)
    if size == 1:
        return values
    even = fft_list(values[0::2], sign)
    odd = fft_list(values[1::2], sign)
    low, high = ([], [])
    for k in range(size // 2):
        (er, ei), (r, i) = (even[k], odd[k])
        if 8 * k == size or 8 * k == 3 * size:
            root = math.sqrt(0.5)
            if 8 * k == size:
                tr, ti = ((r - sign * i) * root, (i + sign * r) * root)
            else:
                tr, ti = ((-r - sign * i) * root, (sign * r - i) * root)
            low.append((er + tr, ei + ti))
            high.append((er - tr, ei - ti))
        elif 4 * k == size:
            if sign > 0:
                low.append((er - i, ei + r))
                high.append((er + i, ei - r))
            else:
                low.append((er + i, ei - r))
                high.append((er - i, ei + r))
        else:
            tr, ti = rotate(r, i, (sign * k, size))
            low.append((er + tr, ei + ti))
            high.append((er - tr, ei - ti))
    return low + high


def times(x, y):
    return (x[0] * y[0] - x[1] * y[1], x[0] * y[1] + x[1] * y[0])


def times_conj(x, y):
    return (x[0] * y[0] + x[1] * y[1], x[1] * y[0] - x[0] * y[1])


def head_kernel(outer, chunk, chunks, steps, a_ref, b_ref, cos_ref, sin_ref, table_ref, out_ref, rows_ref, high_ref, low_ref):
    step = pl.program_id(0)
    cols = rows_ref.shape[1] // 2
    count = outer // chunks
    group = out_ref.shape[0]

    @pl.when(step == 0)
    def _():
        high_ref[...], low_ref[...] = split(table_ref[...])

    @pl.when(step < steps)
    def _():
        for side, src in ((0, a_ref), (cols, b_ref)):
            terms = []
            for r in range(count):
                re = im = None
                for s in range(chunks):
                    at = (r + s * count) * INNER
                    digit = src[:, at : at + INNER].astype(F32)
                    if s == 0:
                        re = digit
                    else:
                        angle = -2.0 * math.pi * s * (4 * chunk + 1) / (4 * chunks)
                        re = re + digit * math.cos(angle)
                        new = digit * math.sin(angle)
                        im = new if im is None else im + new
                angle = -2.0 * math.pi * r * (4 * chunk + 1) / (4 * outer)
                cos, sin = (math.cos(angle), math.sin(angle))
                if im is None:
                    terms.append((re * cos, re * sin))
                elif r == 0:
                    terms.append((re, im))
                else:
                    terms.append((re * cos - im * sin, re * sin + im * cos))
            result = fft_list(terms, -1)
            at = pl.ds(pl.multiple_of(side + step * ROWS_STEP, ROWS_STEP), ROWS_STEP)
            for j in range(count):
                re, im = times_conj(result[j], (cos_ref[j : j + 1, :], sin_ref[j : j + 1, :]))
                rows_ref[j, at, :INNER] = re
                rows_ref[j, at, INNER:] = im

    @pl.when(step >= steps)
    def _():
        table = (high_ref[...], low_ref[...])
        for g in range(group):
            j = (step - steps) * group + g
            if cols % INNER == 0:
                both = three_dot(table, split(rows_ref[j]), ((1,), (1,)))
                sides = (both[:, :cols], both[:, cols:])
            else:
                sides = tuple(
                    three_dot(table, split(rows_ref[j, at : at + cols]), ((1,), (1,))) for at in (0, cols)
                )
            for at in (0, 1):
                out_ref[g, 2 * at] = sides[at][:INNER]
                out_ref[g, 2 * at + 1] = sides[at][INNER:]


def head_stage(limbs_a, limbs_b, cos, sin, table, chunk, chunks):
    cols, length = limbs_a.shape
    outer = length // INNER
    count = outer // chunks
    steps = cols // ROWS_STEP
    group = 2 if count % 2 == 0 else 1
    width = 2 * INNER
    in_spec = pl.BlockSpec((ROWS_STEP, length), lambda i: (jnp.minimum(i, steps - 1), 0))
    turns_spec = pl.BlockSpec((count, INNER), lambda i: (0, 0))
    return pl.pallas_call(
        functools.partial(head_kernel, outer, chunk, chunks, steps),
        grid=(steps + count // group,),
        in_specs=[in_spec, in_spec, turns_spec, turns_spec, pl.BlockSpec((width, width), lambda i: (0, 0))],
        out_specs=pl.BlockSpec((group, 4, INNER, cols), lambda i: (jnp.maximum(i - steps, 0), 0, 0, 0)),
        out_shape=jax.ShapeDtypeStruct((count, 4, INNER, cols), F32),
        scratch_shapes=[pltpu.VMEM((count, 2 * cols, width), F32)] + [pltpu.VMEM((width, width), BF16)] * 2,
        cost_estimate=pl.CostEstimate(
            flops=12 * count * cols * width * width, bytes_accessed=16 * count * cols * width, transcendentals=0
        ),
        name="head_stage",
    )(limbs_a, limbs_b, cos, sin, table)


def middle_kernel(devices, x_ref, ka_cos, ka_sin, q_cos, q_sin, fh, fl, ih, il, v_ref, ya, yb):
    cols = x_ref.shape[3]
    rows = x_ref.shape[2]
    q_turn = (q_cos[...], q_sin[...])

    def turn_of(k):
        return times((ka_cos[k : k + 1, :], ka_sin[k : k + 1, :]), q_turn)

    for at, dst in ((0, ya), (2, yb)):
        result = fft_list([(x_ref[d, at], x_ref[d, at + 1]) for d in range(devices)], -1)
        for k in range(devices):
            re, im = times_conj(result[k], turn_of(k))
            dst[k * rows : (k + 1) * rows, :cols] = re
            dst[k * rows : (k + 1) * rows, cols:] = im
    forward = (fh[...], fl[...])
    inverse = (ih[...], il[...])
    a = three_dot(split(ya[...]), forward, ((1,), (0,)))
    b = three_dot(split(yb[...]), forward, ((1,), (0,)))
    re, im = times((a[:, :cols], a[:, cols:]), (b[:, :cols], b[:, cols:]))
    ya[:, :cols] = re
    ya[:, cols:] = im
    yb[...] = three_dot(split(ya[...]), inverse, ((1,), (0,)))
    terms = []
    for k in range(devices):
        part = slice(k * rows, (k + 1) * rows)
        terms.append(times((yb[part, :cols], yb[part, cols:]), turn_of(k)))
    result = fft_list(terms, 1)
    for d in range(devices):
        v_ref[d, 0] = result[d][0]
        v_ref[d, 1] = result[d][1]


def middle_stage(x, ka_cos, ka_sin, q_cos, q_sin, tables):
    devices, _, count, cols = x.shape
    rows = 8
    whole = lambda t: pl.BlockSpec(t.shape, lambda i: (0, 0))
    q_spec = pl.BlockSpec((rows, cols), lambda i: (i, 0))
    return pl.pallas_call(
        functools.partial(middle_kernel, devices),
        grid=(count // rows,),
        in_specs=[
            pl.BlockSpec((devices, 4, rows, cols), lambda i: (0, 0, i, 0)),
            whole(ka_cos),
            whole(ka_sin),
            q_spec,
            q_spec,
        ]
        + [whole(t) for t in tables],
        out_specs=pl.BlockSpec((devices, 2, rows, cols), lambda i: (0, 0, i, 0)),
        out_shape=jax.ShapeDtypeStruct((devices, 2, count, cols), F32),
        scratch_shapes=[pltpu.VMEM((devices * rows, 2 * cols), F32)] * 2,
        cost_estimate=pl.CostEstimate(
            flops=36 * devices * count * cols * cols * 4, bytes_accessed=24 * devices * count * cols, transcendentals=0
        ),
        name="middle_stage",
    )(x, ka_cos, ka_sin, q_cos, q_sin, *tables)


def tail_kernel(outer, chunk, steps, v_ref, table_ref, cos_ref, sin_ref, *refs):
    *others, out_ref, rows_ref, high_ref, low_ref = refs
    chunks = len(others) + 1
    step = pl.program_id(0)
    count, cols, _ = rows_ref.shape
    group = v_ref.shape[0]

    @pl.when(step == 0)
    def _():
        high_ref[...], low_ref[...] = split(table_ref[...])

    @pl.when(step < steps)
    def _():
        table = (high_ref[...], low_ref[...])
        stacked = jnp.concatenate(
            [jnp.concatenate([v_ref[g, 0].T, v_ref[g, 1].T], axis=1) for g in range(group)], axis=0
        )
        result = three_dot(split(stacked), table, ((1,), (0,)))
        for g in range(group):
            j = step * group + g
            part = result[g * cols : (g + 1) * cols]
            turn = (cos_ref[pl.ds(j, 1), :], sin_ref[pl.ds(j, 1), :])
            re, im = times((part[:, :INNER], part[:, INNER:]), turn)
            rows_ref[j, :, :INNER] = re
            rows_ref[j, :, INNER:] = im

    @pl.when(step >= steps)
    def _():
        at = pl.ds(pl.multiple_of((step - steps) * ROWS_STEP, ROWS_STEP), ROWS_STEP)
        result = fft_list([(rows_ref[j, at, :INNER], rows_ref[j, at, INNER:]) for j in range(count)], 1)
        for r in range(count):
            mine = rotate(*result[r], (r * (4 * chunk + 1), 4 * outer))
            if out_ref.ndim == 3:
                out_ref[r, :, :INNER] = mine[0]
                out_ref[r, :, INNER:] = mine[1]
                continue
            sums = fft_list([(o[r, :, :INNER], o[r, :, INNER:]) for o in others] + [mine], 1)
            for s in range(chunks):
                re, im = rotate(*sums[s], (s, 4 * chunks))
                low = (r + s * count) * INNER
                high = low + outer * INNER
                out_ref[:, low : low + INNER] = re
                out_ref[:, high : high + INNER] = -im


def tail_stage(v, table, cos, sin, others, chunk, chunks):
    count, _, _, cols = v.shape
    outer = count * chunks
    group = 4 if count % 4 == 0 else 1
    width = 2 * INNER
    steps = count // group
    final = chunk == chunks - 1
    later = lambda i: jnp.maximum(i - steps, 0)
    turns_spec = pl.BlockSpec((count, INNER), lambda i: (0, 0))
    row_spec = pl.BlockSpec((count, ROWS_STEP, width), lambda i: (0, later(i), 0))
    if final:
        out_spec = pl.BlockSpec((ROWS_STEP, outer * width), lambda i: (later(i), 0))
        out_shape = jax.ShapeDtypeStruct((cols, outer * width), F32)
    else:
        out_spec = row_spec
        out_shape = jax.ShapeDtypeStruct((count, cols, width), F32)
    others = others if final else []
    return pl.pallas_call(
        functools.partial(tail_kernel, outer, chunk, steps),
        grid=(steps + cols // ROWS_STEP,),
        in_specs=[
            pl.BlockSpec((group, 2, INNER, cols), lambda i: (jnp.minimum(i, steps - 1), 0, 0, 0)),
            pl.BlockSpec((width, width), lambda i: (0, 0)),
            turns_spec,
            turns_spec,
        ]
        + [row_spec] * len(others),
        out_specs=out_spec,
        out_shape=out_shape,
        scratch_shapes=[pltpu.VMEM((count, cols, width), F32)] + [pltpu.VMEM((width, width), BF16)] * 2,
        cost_estimate=pl.CostEstimate(
            flops=6 * count * cols * width * width, bytes_accessed=16 * count * cols * width, transcendentals=0
        ),
        name="tail_stage",
    )(v, table, cos, sin, *others)


def turns(phase, modulus):
    angle = (phase % modulus).astype(F32) * (2.0 * math.pi / modulus)
    return (jnp.cos(angle), jnp.sin(angle))


def iota(shape, dim):
    return lax.broadcasted_iota(jnp.int32, shape, dim)


def row_turns(outer, devices, device, chunk, chunks):
    shape = (outer // chunks, INNER)
    freq = chunks * iota(shape, 0) + chunk
    phase = (4 * freq + 1) * (devices * iota(shape, 1) + device)
    return turns(phase, 4 * outer * INNER * devices)


def row_table(devices, device):
    shape = (2 * INNER, 2 * INNER)
    row, col = (iota(shape, 0), iota(shape, 1))
    modulus = 4 * INNER * devices
    phase = 4 * (row % INNER) * (devices * (col % INNER) + device)
    quarter = INNER * devices * (row // INNER - col // INNER)
    angle = ((phase + quarter) % modulus).astype(F32) * (2.0 * math.pi / modulus)
    return jnp.cos(angle)


def spectral_turns(local, cols, devices, device, outer, total):
    shape = (local, cols)
    at = iota(shape, 0) + device * local
    freq = at // INNER + outer * (at % INNER)
    return turns(iota(shape, 1) * (4 * freq + 1), total)


def np_split(value):
    high = value.astype(np.float32).astype(BF16)
    low = (value - high.astype(np.float64)).astype(np.float32).astype(BF16)
    return (high, low)


def column_tables(cols, devices, scale):
    k = np.arange(devices)[:, None] * np.arange(cols)[None, :]
    angle = 2.0 * np.pi * k / (cols * devices)
    n = np.arange(cols)
    theta = 2.0 * np.pi * (n[:, None] * n[None, :] % cols) / cols
    forward = np.block([[np.cos(theta), -np.sin(theta)], [np.sin(theta), np.cos(theta)]])
    tables = np_split(forward) + np_split(forward.T * scale)
    return (np.cos(angle).astype(np.float32), np.sin(angle).astype(np.float32), tables)


def exchange(value):
    return lax.all_to_all(value, AXES, split_axis=0, concat_axis=0, tiled=True)


def on_device(limbs_a, limbs_b):
    devices = lax.axis_size(AXES)
    device = lax.axis_index(AXES)
    cols, length = limbs_a.shape
    outer = length // INNER
    total = length * cols * devices
    scale = 1.0 / (total * DIGIT_VAR * math.sqrt(total))
    chunks = max(1, outer // devices)
    pieces = max(1, devices // outer)
    local = length // devices
    rows = [row_turns(outer, devices, device, h, chunks) for h in range(chunks)]
    table = row_table(devices, device)
    ka_cos, ka_sin, tables = column_tables(cols, devices, scale)
    q_cos, q_sin = spectral_turns(local, cols, devices, device, outer, 4 * total)
    each = local // chunks

    arrived = []
    for h in range(chunks):
        x = head_stage(limbs_a, limbs_b, *rows[h], table, h, chunks)
        if pieces > 1:
            x = x.reshape(outer, 4, pieces, each, cols).transpose(0, 2, 1, 3, 4)
            x = x.reshape(devices, 4, each, cols)
        arrived.append(exchange(x))
    back = []
    for h in range(chunks):
        part = slice(h * each, (h + 1) * each)
        v = middle_stage(arrived[h], ka_cos, ka_sin, q_cos[part], q_sin[part], tables)
        back.append(exchange(v))
    parts = []
    for h in range(chunks):
        v = back[h]
        if pieces > 1:
            v = v.reshape(outer, pieces, 2, each, cols).transpose(0, 2, 1, 3, 4)
            v = v.reshape(outer, 2, INNER, cols)
        parts.append(tail_stage(v, table, *rows[h], parts, h, chunks))
    return parts[-1]


def solution(mesh):
    placed = P(AXES, None)
    return jax.shard_map(
        on_device, mesh=mesh, in_specs=(placed, placed), out_specs=placed, check_vma=False
    )
```

time: 644 us -> 625 us (0.970)
  Pallas kernels: 125 us -> 112 us
    pallas_call x6 -> x4, Pallas kernels: 87.5 us -> 75.4 us  [the longest x2 43.7 us: head_stage(): pl.pallas_call(functools.partial(head_kernel, outer, chunk, chunks, steps...]
  transfers between devices with their start and end apart: 4 -> 4, of which waited for: 4 -> 4; matrix products, arithmetic and copies ran while one was open for 1% -> 0% of each run, Pallas kernels for 10% -> 12%
where the time goes in v2:
time: 625 us; the launch traced here: 623 us
  waiting for transfers between devices  485 us (78%)
  Pallas kernels  112 us (18%)
  starting transfers between devices  19.9 us (3%)
    all_to_all x4, waiting for transfers between devices, exchange(): return lax.all_to_all(value, AXES, split_axis=0, concat_axis=0, tiled=True)  485 us
    pallas_call x2, Pallas kernels, head_stage(): pl.pallas_call(functools.partial(head_kernel, outer, chunk, chunks, steps...  43.7 us
    pallas_call x2, Pallas kernels, middle_stage(): pl.pallas_call(functools.partial(middle_kernel, devices), grid=(count //...  37 us
    pallas_call x2, Pallas kernels, tail_stage(): pl.pallas_call(functools.partial(tail_kernel, outer, chunk, steps), grid=...  31.6 us
    all_to_all x4, starting transfers between devices, exchange(): return lax.all_to_all(value, AXES, split_axis=0, concat_axis=0, tiled=True)  19.9 us
  transfers between devices with their start and end apart: 4, of which 4 were waited for; matrix products, arithmetic and copies ran while one was open for 0% of the time, Pallas kernels for 12%

profile of v2, /device:TPU:0, one launch (start us, length us, event | category | flops | bytes accessed | tf_op | source)
XLA Modules:
  0.0 622.6 jit_solution(14102262466354677346)
XLA Ops:
  0.1 0.8 fusion.15
  0.9 2.0 fusion.3.table_ref
  2.9 21.9 %head_stage.3 = f32[32,4,128,128]{3,2,1,0:T(8,128)} custom-call(s32[128,8192]{1,0:T(8,128)} %a_ref.3, s32[128,8192]{1,0:T(8,128)} %b_ref.3, f32[32,128]{1,0:T(8,128)} %get-tuple-element.12.cos_ref, f32[32,128]{1,0:T(8,128)} %get-tuple-element.11.sin_ref, f32[256,256]{1,0:T(8,128)} %fusion.3.table_ref), custom_call_target="tpu_custom_call" | custom-call | flops 3221225472 | bytes 16777216 | tf_op jit(solution)/shard_map/head_stage/pallas_call | solution.py:156
  24.8 7.5 %all-to-all-start.2 = ((f32[32,4,128,128]{3,2,1,0:T(8,128)}), f32[32,4,128,128]{3,2,1,0:T(8,128)}, u32[]{:S(2)}, u32[]{:S(2)}) async-start(f32[32,4,128,128]{3,2,1,0:T(8,128)} %head_stage.3), calls=%async_computation.2 | async-start | bytes 16777216 | tf_op jit(solution)/shard_map/all_to_all | solution.py:360
  32.3 21.8 %head_stage.2 = f32[32,4,128,128]{3,2,1,0:T(8,128)} custom-call(s32[128,8192]{1,0:T(8,128)} %a_ref.3, s32[128,8192]{1,0:T(8,128)} %b_ref.3, f32[32,128]{1,0:T(8,128)} %get-tuple-element.15.cos_ref, f32[32,128]{1,0:T(8,128)} %get-tuple-element.16.sin_ref, f32[256,256]{1,0:T(8,128)} %fusion.3.table_ref), custom_call_target="tpu_custom_call" | custom-call | flops 3221225472 | bytes 16777216 | tf_op jit(solution)/shard_map/head_stage/pallas_call | solution.py:156
  54.1 164.3 %all-to-all-done.2.x_ref = f32[32,4,128,128]{3,2,1,0:T(8,128)} async-done(((f32[32,4,128,128]{3,2,1,0:T(8,128)}), f32[32,4,128,128]{3,2,1,0:T(8,128)}, u32[]{:S(2)}, u32[]{:S(2)}) %all-to-all-start.2) | async-done | bytes 8388640 | tf_op jit(solution)/shard_map/all_to_all | solution.py:360
  218.4 4.4 all-to-all-start
  222.8 0.6 fusion.7
  223.5 0.7 fusion.22
  224.1 0.7 fusion.23
  224.8 18.5 %middle_stage.3 = f32[32,2,128,128]{3,2,1,0:T(8,128)} custom-call(f32[32,4,128,128]{3,2,1,0:T(8,128)} %all-to-all-done.2.x_ref, f32[32,128]{1,0:T(8,128)} %constant.151.clone.ka_cos, f32[32,128]{1,0:T(8,128)} %constant.152.clone.ka_sin, f32[128,128]{1,0:T(8,128)} %get-tuple-element.7.q_cos, f32[128,128]{1,0:T(8,128)} %get-tuple-element.5.q_sin, ...), custom_call_target="tpu_custom_call" | custom-call | flops 9663676416 | bytes 12582912 | tf_op jit(solution)/shard_map/middle_stage/pallas_call | solution.py:207
  243.3 165.5 %all-to-all-done.x_ref = f32[32,4,128,128]{3,2,1,0:T(8,128)} async-done(((f32[32,4,128,128]{3,2,1,0:T(8,128)}), f32[32,4,128,128]{3,2,1,0:T(8,128)}, u32[]{:S(2)}, u32[]{:S(2)}) %all-to-all-start) | async-done | bytes 8388640 | tf_op jit(solution)/shard_map/all_to_all | solution.py:360
  408.8 4.4 all-to-all-start.3
  413.2 18.5 %middle_stage.2 = f32[32,2,128,128]{3,2,1,0:T(8,128)} custom-call(f32[32,4,128,128]{3,2,1,0:T(8,128)} %all-to-all-done.x_ref, f32[32,128]{1,0:T(8,128)} %constant.151.clone.ka_cos, f32[32,128]{1,0:T(8,128)} %constant.152.clone.ka_sin, f32[128,128]{1,0:T(8,128)} %get-tuple-element.8.q_cos, f32[128,128]{1,0:T(8,128)} %get-tuple-element.6.q_sin, ...), custom_call_target="tpu_custom_call" | custom-call | flops 9663676416 | bytes 12582912 | tf_op jit(solution)/shard_map/middle_stage/pallas_call | solution.py:207
  431.7 75.4 %all-to-all-done.3.v_ref = f32[32,2,128,128]{3,2,1,0:T(8,128)} async-done(((f32[32,2,128,128]{3,2,1,0:T(8,128)}), f32[32,2,128,128]{3,2,1,0:T(8,128)}, u32[]{:S(2)}, u32[]{:S(2)}) %all-to-all-start.3) | async-done | bytes 4194336 | tf_op jit(solution)/shard_map/all_to_all | solution.py:360
  507.1 3.7 all-to-all-start.1
  510.8 13.7 %tail_stage.2.refs_0_ = f32[32,128,256]{2,1,0:T(8,128)} custom-call(f32[32,2,128,128]{3,2,1,0:T(8,128)} %all-to-all-done.3.v_ref, f32[256,256]{1,0:T(8,128)} %fusion.3.table_ref, f32[32,128]{1,0:T(8,128)} %get-tuple-element.12.cos_ref, f32[32,128]{1,0:T(8,128)} %get-tuple-element.11.sin_ref), custom_call_target="tpu_custom_call" | custom-call | flops 1610612736 | bytes 16777216 | tf_op jit(solution)/shard_map/tail_stage/pallas_call | solution.py:290
  524.4 80.2 %all-to-all-done.1.v_ref = f32[32,2,128,128]{3,2,1,0:T(8,128)} async-done(((f32[32,2,128,128]{3,2,1,0:T(8,128)}), f32[32,2,128,128]{3,2,1,0:T(8,128)}, u32[]{:S(2)}, u32[]{:S(2)}) %all-to-all-start.1) | async-done | bytes 4194336 | tf_op jit(solution)/shard_map/all_to_all | solution.py:360
  604.6 18.0 %tail_stage.3 = f32[128,16384]{1,0:T(8,128)} custom-call(f32[32,2,128,128]{3,2,1,0:T(8,128)} %all-to-all-done.1.v_ref, f32[256,256]{1,0:T(8,128)} %fusion.3.table_ref, f32[32,128]{1,0:T(8,128)} %get-tuple-element.15.cos_ref, f32[32,128]{1,0:T(8,128)} %get-tuple-element.16.sin_ref, f32[32,128,256]{2,1,0:T(8,128)} %tail_stage.2.refs_0_), custom_call_target="tpu_custom_call" | custom-call | flops 1610612736 | bytes 16777216 | tf_op jit(solution)/shard_map/tail_stage/pallas_call | solution.py:290
  (8 shorter events, 0.1 us)
Async XLA Ops:
  24.8 193.5 %all-to-all-start.2 = ((f32[32,4,128,128]{3,2,1,0:T(8,128)}), f32[32,4,128,128]{3,2,1,0:T(8,128)}, u32[]{:S(2)}, u32[]{:S(2)}) async-start(f32[32,4,128,128]{3,2,1,0:T(8,128)} %head_stage.3), calls=%async_computation.2 | async-start | bytes 16777216 | tf_op jit(solution)/shard_map/all_to_all | solution.py:360
  218.4 190.5 %all-to-all-start = ((f32[32,4,128,128]{3,2,1,0:T(8,128)}), f32[32,4,128,128]{3,2,1,0:T(8,128)}, u32[]{:S(2)}, u32[]{:S(2)}) async-start(f32[32,4,128,128]{3,2,1,0:T(8,128)} %head_stage.2), calls=%async_computation | async-start | bytes 16777216 | tf_op jit(solution)/shard_map/all_to_all | solution.py:360
  408.8 98.3 %all-to-all-start.3 = ((f32[32,2,128,128]{3,2,1,0:T(8,128)}), f32[32,2,128,128]{3,2,1,0:T(8,128)}, u32[]{:S(2)}, u32[]{:S(2)}) async-start(f32[32,2,128,128]{3,2,1,0:T(8,128)} %middle_stage.3), calls=%async_computation.3 | async-start | bytes 8388608 | tf_op jit(solution)/shard_map/all_to_all | solution.py:360
  507.1 97.5 %all-to-all-start.1 = ((f32[32,2,128,128]{3,2,1,0:T(8,128)}), f32[32,2,128,128]{3,2,1,0:T(8,128)}, u32[]{:S(2)}, u32[]{:S(2)}) async-start(f32[32,2,128,128]{3,2,1,0:T(8,128)} %middle_stage.2), calls=%async_computation.1 | async-start | bytes 8388608 | tf_op jit(solution)/shard_map/all_to_all | solution.py:360

commit v3 on v2

--- a/solution.py
+++ b/solution.py
@@ -11,7 +11,11 @@
 
 DIGIT_VAR = 5461.25
 INNER = 128
-ROWS_STEP = 8
+SUBLANES = 8
+HEAD_ROWS = 32
+HEAD_GROUP = 4
+TAIL_ROWS = 64
+TAIL_GROUP = 16
 AXES = ("fft", "grp")
 BF16 = jnp.bfloat16
 F32 = jnp.float32
@@ -86,6 +90,32 @@
     return (x[0] * y[0] + x[1] * y[1], x[1] * y[0] - x[0] * y[1])
 
 
+def head_terms(src, own, outer, chunk, chunks):
+    count = outer // chunks
+    terms = []
+    for r in range(count):
+        re = im = None
+        for s in range(chunks):
+            at = (r + s * count) * INNER
+            digit = src[own, at : at + INNER].astype(F32)
+            if s == 0:
+                re = digit
+            else:
+                angle = -2.0 * math.pi * s * (4 * chunk + 1) / (4 * chunks)
+                re = re + digit * math.cos(angle)
+                new = digit * math.sin(angle)
+                im = new if im is None else im + new
+        angle = -2.0 * math.pi * r * (4 * chunk + 1) / (4 * outer)
+        cos, sin = (math.cos(angle), math.sin(angle))
+        if im is None:
+            terms.append((re * cos, re * sin))
+        elif r == 0:
+            terms.append((re, im))
+        else:
+            terms.append((re * cos - im * sin, re * sin + im * cos))
+    return terms
+
+
 def head_kernel(outer, chunk, chunks, steps, a_ref, b_ref, cos_ref, sin_ref, table_ref, out_ref, rows_ref, high_ref, low_ref):
     step = pl.program_id(0)
     cols = rows_ref.shape[1] // 2
@@ -98,39 +128,25 @@
 
     @pl.when(step < steps)
     def _():
-        for side, src in ((0, a_ref), (cols, b_ref)):
-            terms = []
-            for r in range(count):
-                re = im = None
-                for s in range(chunks):
-                    at = (r + s * count) * INNER
-                    digit = src[:, at : at + INNER].astype(F32)
-                    if s == 0:
-                        re = digit
-                    else:
-                        angle = -2.0 * math.pi * s * (4 * chunk + 1) / (4 * chunks)
-                        re = re + digit * math.cos(angle)
-                        new = digit * math.sin(angle)
-                        im = new if im is None else im + new
-                angle = -2.0 * math.pi * r * (4 * chunk + 1) / (4 * outer)
-                cos, sin = (math.cos(angle), math.sin(angle))
-                if im is None:
-                    terms.append((re * cos, re * sin))
-                elif r == 0:
-                    terms.append((re, im))
-                else:
-                    terms.append((re * cos - im * sin, re * sin + im * cos))
-            result = fft_list(terms, -1)
-            at = pl.ds(pl.multiple_of(side + step * ROWS_STEP, ROWS_STEP), ROWS_STEP)
-            for j in range(count):
-                re, im = times_conj(result[j], (cos_ref[j : j + 1, :], sin_ref[j : j + 1, :]))
-                rows_ref[j, at, :INNER] = re
-                rows_ref[j, at, INNER:] = im
+        tile_rows = a_ref.shape[0]
+
+        @pl.loop(0, tile_rows // SUBLANES)
+        def _(i):
+            own = pl.ds(pl.multiple_of(i * SUBLANES, SUBLANES), SUBLANES)
+            for side, src in ((0, a_ref), (cols, b_ref)):
+                terms = head_terms(src, own, outer, chunk, chunks)
+                result = fft_list(terms, -1)
+                at = pl.ds(pl.multiple_of(side + step * tile_rows + i * SUBLANES, SUBLANES), SUBLANES)
+                for j in range(count):
+                    re, im = times_conj(result[j], (cos_ref[j : j + 1, :], sin_ref[j : j + 1, :]))
+                    rows_ref[j, at, :INNER] = re
+                    rows_ref[j, at, INNER:] = im
 
     @pl.when(step >= steps)
     def _():
         table = (high_ref[...], low_ref[...])
-        for g in range(group):
+        @pl.loop(0, group)
+        def _(g):
             j = (step - steps) * group + g
             if cols % INNER == 0:
                 both = three_dot(table, split(rows_ref[j]), ((1,), (1,)))
@@ -148,10 +164,11 @@
     cols, length = limbs_a.shape
     outer = length // INNER
     count = outer // chunks
-    steps = cols // ROWS_STEP
-    group = 2 if count % 2 == 0 else 1
+    tile_rows = min(cols, HEAD_ROWS)
+    steps = cols // tile_rows
+    group = math.gcd(count, HEAD_GROUP)
     width = 2 * INNER
-    in_spec = pl.BlockSpec((ROWS_STEP, length), lambda i: (jnp.minimum(i, steps - 1), 0))
+    in_spec = pl.BlockSpec((tile_rows, length), lambda i: (jnp.minimum(i, steps - 1), 0))
     turns_spec = pl.BlockSpec((count, INNER), lambda i: (0, 0))
     return pl.pallas_call(
         functools.partial(head_kernel, outer, chunk, chunks, steps),
@@ -230,7 +247,7 @@
     chunks = len(others) + 1
     step = pl.program_id(0)
     count, cols, _ = rows_ref.shape
-    group = v_ref.shape[0]
+    group = min(v_ref.shape[0], 4)
 
     @pl.when(step == 0)
     def _():
@@ -239,49 +256,61 @@
     @pl.when(step < steps)
     def _():
         table = (high_ref[...], low_ref[...])
-        stacked = jnp.concatenate(
-            [jnp.concatenate([v_ref[g, 0].T, v_ref[g, 1].T], axis=1) for g in range(group)], axis=0
-        )
-        result = three_dot(split(stacked), table, ((1,), (0,)))
-        for g in range(group):
-            j = step * group + g
-            part = result[g * cols : (g + 1) * cols]
-            turn = (cos_ref[pl.ds(j, 1), :], sin_ref[pl.ds(j, 1), :])
-            re, im = times((part[:, :INNER], part[:, INNER:]), turn)
-            rows_ref[j, :, :INNER] = re
-            rows_ref[j, :, INNER:] = im
+        @pl.loop(0, v_ref.shape[0] // group)
+        def _(i):
+            stacked = jnp.concatenate(
+                [
+                    jnp.concatenate([v_ref[i * group + g, p].T for p in (0, 1)], axis=1)
+                    for g in range(group)
+                ],
+                axis=0,
+            )
+            result = three_dot(split(stacked), table, ((1,), (0,)))
+            for g in range(group):
+                j = step * v_ref.shape[0] + i * group + g
+                part = result[g * cols : (g + 1) * cols]
+                turn = (cos_ref[pl.ds(j, 1), :], sin_ref[pl.ds(j, 1), :])
+                re, im = times((part[:, :INNER], part[:, INNER:]), turn)
+                rows_ref[j, :, :INNER] = re
+                rows_ref[j, :, INNER:] = im
 
     @pl.when(step >= steps)
     def _():
-        at = pl.ds(pl.multiple_of((step - steps) * ROWS_STEP, ROWS_STEP), ROWS_STEP)
-        result = fft_list([(rows_ref[j, at, :INNER], rows_ref[j, at, INNER:]) for j in range(count)], 1)
-        for r in range(count):
-            mine = rotate(*result[r], (r * (4 * chunk + 1), 4 * outer))
-            if out_ref.ndim == 3:
-                out_ref[r, :, :INNER] = mine[0]
-                out_ref[r, :, INNER:] = mine[1]
-                continue
-            sums = fft_list([(o[r, :, :INNER], o[r, :, INNER:]) for o in others] + [mine], 1)
-            for s in range(chunks):
-                re, im = rotate(*sums[s], (s, 4 * chunks))
-                low = (r + s * count) * INNER
-                high = low + outer * INNER
-                out_ref[:, low : low + INNER] = re
-                out_ref[:, high : high + INNER] = -im
+        tile_rows = out_ref.shape[-2]
+
+        @pl.loop(0, tile_rows // SUBLANES)
+        def _(i):
+            own = pl.ds(pl.multiple_of(i * SUBLANES, SUBLANES), SUBLANES)
+            at = pl.ds(pl.multiple_of((step - steps) * tile_rows + i * SUBLANES, SUBLANES), SUBLANES)
+            result = fft_list([(rows_ref[j, at, :INNER], rows_ref[j, at, INNER:]) for j in range(count)], 1)
+            for r in range(count):
+                mine = rotate(*result[r], (r * (4 * chunk + 1), 4 * outer))
+                if out_ref.ndim == 3:
+                    out_ref[r, own, :INNER] = mine[0]
+                    out_ref[r, own, INNER:] = mine[1]
+                    continue
+                sums = fft_list([(o[r, own, :INNER], o[r, own, INNER:]) for o in others] + [mine], 1)
+                for s in range(chunks):
+                    re, im = rotate(*sums[s], (s, 4 * chunks))
+                    low = (r + s * count) * INNER
+                    high = low + outer * INNER
+                    out_ref[own, low : low + INNER] = re
+                    out_ref[own, high : high + INNER] = -im
 
 
 def tail_stage(v, table, cos, sin, others, chunk, chunks):
     count, _, _, cols = v.shape
     outer = count * chunks
-    group = 4 if count % 4 == 0 else 1
+    group = math.gcd(count, TAIL_GROUP)
+    tile_rows = min(cols, TAIL_ROWS)
     width = 2 * INNER
     steps = count // group
     final = chunk == chunks - 1
     later = lambda i: jnp.maximum(i - steps, 0)
     turns_spec = pl.BlockSpec((count, INNER), lambda i: (0, 0))
-    row_spec = pl.BlockSpec((count, ROWS_STEP, width), lambda i: (0, later(i), 0))
+    row_spec = pl.BlockSpec((count, tile_rows, width), lambda i: (0, later(i), 0))
     if final:
-        out_spec = pl.BlockSpec((ROWS_STEP, outer * width), lambda i: (later(i), 0))
+        out_spec = pl.BlockSpec((tile_rows, outer * width), lambda i: (later(i), 0))
         out_shape = jax.ShapeDtypeStruct((cols, outer * width), F32)
     else:
         out_spec = row_spec
@@ -289,7 +318,7 @@
     others = others if final else []
     return pl.pallas_call(
         functools.partial(tail_kernel, outer, chunk, steps),
-        grid=(steps + cols // ROWS_STEP,),
+        grid=(steps + cols // tile_rows,),
         in_specs=[
             pl.BlockSpec((group, 2, INNER, cols), lambda i: (jnp.minimum(i, steps - 1), 0, 0, 0)),
             pl.BlockSpec((width, width), lambda i: (0, 0)),

time: 625 us -> 613 us (0.981)
  Pallas kernels: 112 us -> 92.6 us
  waiting for transfers between devices: 485 us -> 494 us
    pallas_call x2, Pallas kernels: 31.6 us -> 19 us  [tail_stage(): pl.pallas_call(functools.partial(tail_kernel, outer, chunk, steps), grid=...]
    all_to_all x4, waiting for transfers between devices: 485 us -> 494 us  [exchange(): return lax.all_to_all(value, AXES, split_axis=0, concat_axis=0, tiled=True)]
    pallas_call x2, Pallas kernels: 43.7 us -> 36.6 us  [head_stage(): pl.pallas_call(functools.partial(head_kernel, outer, chunk, chunks, steps...]
  transfers between devices with their start and end apart: 4 -> 4, of which waited for: 4 -> 4; matrix products, arithmetic and copies ran while one was open for 0% -> 0% of each run, Pallas kernels for 12% -> 10%
where the time goes in v3:
time: 613 us; the launch traced here: 612 us
  waiting for transfers between devices  494 us (81%)
  Pallas kernels  92.6 us (15%)
  starting transfers between devices  19.9 us (3%)
    all_to_all x4, waiting for transfers between devices, exchange(): return lax.all_to_all(value, AXES, split_axis=0, concat_axis=0, tiled=True)  494 us
    pallas_call x2, Pallas kernels, middle_stage(): pl.pallas_call(functools.partial(middle_kernel, devices), grid=(count //...  37 us
    pallas_call x2, Pallas kernels, head_stage(): pl.pallas_call(functools.partial(head_kernel, outer, chunk, chunks, steps...  36.6 us
    all_to_all x4, starting transfers between devices, exchange(): return lax.all_to_all(value, AXES, split_axis=0, concat_axis=0, tiled=True)  19.9 us
    pallas_call x2, Pallas kernels, tail_stage(): pl.pallas_call(functools.partial(tail_kernel, outer, chunk, steps), grid=...  19 us
  transfers between devices with their start and end apart: 4, of which 4 were waited for; matrix products, arithmetic and copies ran while one was open for 0% of the time, Pallas kernels for 10%

profile of v3, /device:TPU:0, one launch (start us, length us, event | category | flops | bytes accessed | tf_op | source)
XLA Modules:
  0.0 611.7 jit_solution(7137278046611868673)
XLA Ops:
  0.1 0.8 fusion.15
  0.9 2.0 fusion.3.table_ref
  2.9 18.3 %head_stage.3 = f32[32,4,128,128]{3,2,1,0:T(8,128)} custom-call(s32[128,8192]{1,0:T(8,128)} %a_ref.3, s32[128,8192]{1,0:T(8,128)} %b_ref.3, f32[32,128]{1,0:T(8,128)} %get-tuple-element.12.cos_ref, f32[32,128]{1,0:T(8,128)} %get-tuple-element.11.sin_ref, f32[256,256]{1,0:T(8,128)} %fusion.3.table_ref), custom_call_target="tpu_custom_call" | custom-call | flops 3221225472 | bytes 16777216 | tf_op jit(solution)/shard_map/head_stage/pallas_call | solution.py:173
  21.2 7.5 %all-to-all-start.2 = ((f32[32,4,128,128]{3,2,1,0:T(8,128)}), f32[32,4,128,128]{3,2,1,0:T(8,128)}, u32[]{:S(2)}, u32[]{:S(2)}) async-start(f32[32,4,128,128]{3,2,1,0:T(8,128)} %head_stage.3), calls=%async_computation.2 | async-start | bytes 16777216 | tf_op jit(solution)/shard_map/all_to_all | solution.py:389
  28.7 18.3 %head_stage.2 = f32[32,4,128,128]{3,2,1,0:T(8,128)} custom-call(s32[128,8192]{1,0:T(8,128)} %a_ref.3, s32[128,8192]{1,0:T(8,128)} %b_ref.3, f32[32,128]{1,0:T(8,128)} %get-tuple-element.15.cos_ref, f32[32,128]{1,0:T(8,128)} %get-tuple-element.16.sin_ref, f32[256,256]{1,0:T(8,128)} %fusion.3.table_ref), custom_call_target="tpu_custom_call" | custom-call | flops 3221225472 | bytes 16777216 | tf_op jit(solution)/shard_map/head_stage/pallas_call | solution.py:173
  46.9 167.8 %all-to-all-done.2.x_ref = f32[32,4,128,128]{3,2,1,0:T(8,128)} async-done(((f32[32,4,128,128]{3,2,1,0:T(8,128)}), f32[32,4,128,128]{3,2,1,0:T(8,128)}, u32[]{:S(2)}, u32[]{:S(2)}) %all-to-all-start.2) | async-done | bytes 8388640 | tf_op jit(solution)/shard_map/all_to_all | solution.py:389
  214.7 4.4 all-to-all-start
  219.2 0.6 fusion.7
  219.8 0.7 fusion.22
  220.5 0.7 fusion.23
  221.2 18.5 %middle_stage.3 = f32[32,2,128,128]{3,2,1,0:T(8,128)} custom-call(f32[32,4,128,128]{3,2,1,0:T(8,128)} %all-to-all-done.2.x_ref, f32[32,128]{1,0:T(8,128)} %constant.151.clone.ka_cos, f32[32,128]{1,0:T(8,128)} %constant.152.clone.ka_sin, f32[128,128]{1,0:T(8,128)} %get-tuple-element.7.q_cos, f32[128,128]{1,0:T(8,128)} %get-tuple-element.5.q_sin, ...), custom_call_target="tpu_custom_call" | custom-call | flops 9663676416 | bytes 12582912 | tf_op jit(solution)/shard_map/middle_stage/pallas_call | solution.py:224
  239.7 165.5 %all-to-all-done.x_ref = f32[32,4,128,128]{3,2,1,0:T(8,128)} async-done(((f32[32,4,128,128]{3,2,1,0:T(8,128)}), f32[32,4,128,128]{3,2,1,0:T(8,128)}, u32[]{:S(2)}, u32[]{:S(2)}) %all-to-all-start) | async-done | bytes 8388640 | tf_op jit(solution)/shard_map/all_to_all | solution.py:389
  405.2 4.4 all-to-all-start.3
  409.6 18.5 %middle_stage.2 = f32[32,2,128,128]{3,2,1,0:T(8,128)} custom-call(f32[32,4,128,128]{3,2,1,0:T(8,128)} %all-to-all-done.x_ref, f32[32,128]{1,0:T(8,128)} %constant.151.clone.ka_cos, f32[32,128]{1,0:T(8,128)} %constant.152.clone.ka_sin, f32[128,128]{1,0:T(8,128)} %get-tuple-element.8.q_cos, f32[128,128]{1,0:T(8,128)} %get-tuple-element.6.q_sin, ...), custom_call_target="tpu_custom_call" | custom-call | flops 9663676416 | bytes 12582912 | tf_op jit(solution)/shard_map/middle_stage/pallas_call | solution.py:224
  428.1 75.4 %all-to-all-done.3.v_ref = f32[32,2,128,128]{3,2,1,0:T(8,128)} async-done(((f32[32,2,128,128]{3,2,1,0:T(8,128)}), f32[32,2,128,128]{3,2,1,0:T(8,128)}, u32[]{:S(2)}, u32[]{:S(2)}) %all-to-all-start.3) | async-done | bytes 4194336 | tf_op jit(solution)/shard_map/all_to_all | solution.py:389
  503.5 3.7 all-to-all-start.1
  507.2 8.4 %tail_stage.2.refs_0_ = f32[32,128,256]{2,1,0:T(8,128)} custom-call(f32[32,2,128,128]{3,2,1,0:T(8,128)} %all-to-all-done.3.v_ref, f32[256,256]{1,0:T(8,128)} %fusion.3.table_ref, f32[32,128]{1,0:T(8,128)} %get-tuple-element.12.cos_ref, f32[32,128]{1,0:T(8,128)} %get-tuple-element.11.sin_ref), custom_call_target="tpu_custom_call" | custom-call | flops 1610612736 | bytes 16777216 | tf_op jit(solution)/shard_map/tail_stage/pallas_call | solution.py:319
  515.5 85.5 %all-to-all-done.1.v_ref = f32[32,2,128,128]{3,2,1,0:T(8,128)} async-done(((f32[32,2,128,128]{3,2,1,0:T(8,128)}), f32[32,2,128,128]{3,2,1,0:T(8,128)}, u32[]{:S(2)}, u32[]{:S(2)}) %all-to-all-start.1) | async-done | bytes 4194336 | tf_op jit(solution)/shard_map/all_to_all | solution.py:389
  601.0 10.6 %tail_stage.3 = f32[128,16384]{1,0:T(8,128)} custom-call(f32[32,2,128,128]{3,2,1,0:T(8,128)} %all-to-all-done.1.v_ref, f32[256,256]{1,0:T(8,128)} %fusion.3.table_ref, f32[32,128]{1,0:T(8,128)} %get-tuple-element.15.cos_ref, f32[32,128]{1,0:T(8,128)} %get-tuple-element.16.sin_ref, f32[32,128,256]{2,1,0:T(8,128)} %tail_stage.2.refs_0_), custom_call_target="tpu_custom_call" | custom-call | flops 1610612736 | bytes 16777216 | tf_op jit(solution)/shard_map/tail_stage/pallas_call | solution.py:319
  (8 shorter events, 0.1 us)
Async XLA Ops:
  21.2 193.5 %all-to-all-start.2 = ((f32[32,4,128,128]{3,2,1,0:T(8,128)}), f32[32,4,128,128]{3,2,1,0:T(8,128)}, u32[]{:S(2)}, u32[]{:S(2)}) async-start(f32[32,4,128,128]{3,2,1,0:T(8,128)} %head_stage.3), calls=%async_computation.2 | async-start | bytes 16777216 | tf_op jit(solution)/shard_map/all_to_all | solution.py:389
  214.7 190.5 %all-to-all-start = ((f32[32,4,128,128]{3,2,1,0:T(8,128)}), f32[32,4,128,128]{3,2,1,0:T(8,128)}, u32[]{:S(2)}, u32[]{:S(2)}) async-start(f32[32,4,128,128]{3,2,1,0:T(8,128)} %head_stage.2), calls=%async_computation | async-start | bytes 16777216 | tf_op jit(solution)/shard_map/all_to_all | solution.py:389
  405.2 98.3 %all-to-all-start.3 = ((f32[32,2,128,128]{3,2,1,0:T(8,128)}), f32[32,2,128,128]{3,2,1,0:T(8,128)}, u32[]{:S(2)}, u32[]{:S(2)}) async-start(f32[32,2,128,128]{3,2,1,0:T(8,128)} %middle_stage.3), calls=%async_computation.3 | async-start | bytes 8388608 | tf_op jit(solution)/shard_map/all_to_all | solution.py:389
  503.5 97.5 %all-to-all-start.1 = ((f32[32,2,128,128]{3,2,1,0:T(8,128)}), f32[32,2,128,128]{3,2,1,0:T(8,128)}, u32[]{:S(2)}, u32[]{:S(2)}) async-start(f32[32,2,128,128]{3,2,1,0:T(8,128)} %middle_stage.2), calls=%async_computation.1 | async-start | bytes 8388608 | tf_op jit(solution)/shard_map/all_to_all | solution.py:389

commit v4 on v3

--- a/solution.py
+++ b/solution.py
@@ -16,6 +16,7 @@
 HEAD_GROUP = 4
 TAIL_ROWS = 64
 TAIL_GROUP = 16
+MIDDLE_ROWS = 8
 AXES = ("fft", "grp")
 BF16 = jnp.bfloat16
 F32 = jnp.float32
@@ -116,15 +117,23 @@
     return terms
 
 
-def head_kernel(outer, chunk, chunks, steps, a_ref, b_ref, cos_ref, sin_ref, table_ref, out_ref, rows_ref, high_ref, low_ref):
+def head_kernel(
+    outer, classes, chunks, steps, devices, device_ref, a_ref, b_ref, out_ref, rows_ref, high_ref, low_ref, cos_ref, sin_ref
+):
     step = pl.program_id(0)
     cols = rows_ref.shape[1] // 2
     count = outer // chunks
-    group = out_ref.shape[0]
+    pieces = devices // count
+    each = INNER // pieces
+    group = out_ref.shape[0] // pieces
 
     @pl.when(step == 0)
     def _():
-        high_ref[...], low_ref[...] = split(table_ref[...])
+        device = device_ref[0]
+        high_ref[...], low_ref[...] = split(row_table(devices, device))
+        for n, chunk in enumerate(classes):
+            at = slice(n * count, (n + 1) * count)
+            cos_ref[at, :], sin_ref[at, :] = row_turns(outer, devices, device, chunk, chunks)
 
     @pl.when(step < steps)
     def _():
@@ -134,17 +143,19 @@
         def _(i):
             own = pl.ds(pl.multiple_of(i * SUBLANES, SUBLANES), SUBLANES)
             for side, src in ((0, a_ref), (cols, b_ref)):
-                terms = head_terms(src, own, outer, chunk, chunks)
-                result = fft_list(terms, -1)
                 at = pl.ds(pl.multiple_of(side + step * tile_rows + i * SUBLANES, SUBLANES), SUBLANES)
-                for j in range(count):
-                    re, im = times_conj(result[j], (cos_ref[j : j + 1, :], sin_ref[j : j + 1, :]))
-                    rows_ref[j, at, :INNER] = re
-                    rows_ref[j, at, INNER:] = im
+                for n, chunk in enumerate(classes):
+                    result = fft_list(head_terms(src, own, outer, chunk, chunks), -1)
+                    for e in range(count):
+                        j = n * count + e
+                        re, im = times_conj(result[e], (cos_ref[j : j + 1, :], sin_ref[j : j + 1, :]))
+                        rows_ref[j, at, :INNER] = re
+                        rows_ref[j, at, INNER:] = im
 
     @pl.when(step >= steps)
     def _():
         table = (high_ref[...], low_ref[...])
+
         @pl.loop(0, group)
         def _(g):
             j = (step - steps) * group + g
@@ -155,33 +166,44 @@
                 sides = tuple(
                     three_dot(table, split(rows_ref[j, at : at + cols]), ((1,), (1,))) for at in (0, cols)
                 )
-            for at in (0, 1):
-                out_ref[g, 2 * at] = sides[at][:INNER]
-                out_ref[g, 2 * at + 1] = sides[at][INNER:]
-
-
-def head_stage(limbs_a, limbs_b, cos, sin, table, chunk, chunks):
+            for p in range(pieces):
+                for at in (0, 1):
+                    for part in (0, 1):
+                        low = part * INNER + p * each
+                        out_ref[g * pieces + p, 2 * at + part] = sides[at][low : low + each]
+
+
+def head_stage(limbs_a, limbs_b, device, devices, classes, chunks):
     cols, length = limbs_a.shape
     outer = length // INNER
     count = outer // chunks
+    pieces = devices // count
     tile_rows = min(cols, HEAD_ROWS)
     steps = cols // tile_rows
     group = math.gcd(count, HEAD_GROUP)
+    blocks = count // group
     width = 2 * INNER
+    total = len(classes) * count
+    later = lambda i: jnp.maximum(i - steps, 0)
     in_spec = pl.BlockSpec((tile_rows, length), lambda i: (jnp.minimum(i, steps - 1), 0))
-    turns_spec = pl.BlockSpec((count, INNER), lambda i: (0, 0))
+    out_spec = pl.BlockSpec(
+        (group * pieces, None, 4, INNER // pieces, cols),
+        lambda i: (later(i) % blocks, later(i) // blocks, 0, 0, 0),
+    )
     return pl.pallas_call(
-        functools.partial(head_kernel, outer, chunk, chunks, steps),
-        grid=(steps + count // group,),
-        in_specs=[in_spec, in_spec, turns_spec, turns_spec, pl.BlockSpec((width, width), lambda i: (0, 0))],
-        out_specs=pl.BlockSpec((group, 4, INNER, cols), lambda i: (jnp.maximum(i - steps, 0), 0, 0, 0)),
-        out_shape=jax.ShapeDtypeStruct((count, 4, INNER, cols), F32),
-        scratch_shapes=[pltpu.VMEM((count, 2 * cols, width), F32)] + [pltpu.VMEM((width, width), BF16)] * 2,
+        functools.partial(head_kernel, outer, classes, chunks, steps, devices),
+        grid=(steps + len(classes) * blocks,),
+        in_specs=[pl.BlockSpec(memory_space=pltpu.SMEM), in_spec, in_spec],
+        out_specs=out_spec,
+        out_shape=jax.ShapeDtypeStruct((devices, len(classes), 4, INNER // pieces, cols), F32),
+        scratch_shapes=[pltpu.VMEM((total, 2 * cols, width), F32)]
+        + [pltpu.VMEM((width, width), BF16)] * 2
+        + [pltpu.VMEM((total, INNER), F32)] * 2,
         cost_estimate=pl.CostEstimate(
-            flops=12 * count * cols * width * width, bytes_accessed=16 * count * cols * width, transcendentals=0
+            flops=12 * total * cols * width * width, bytes_accessed=16 * total * cols * width, transcendentals=0
         ),
         name="head_stage",
-    )(limbs_a, limbs_b, cos, sin, table)
+    )(device, limbs_a, limbs_b)
 
 
 def middle_kernel(devices, x_ref, ka_cos, ka_sin, q_cos, q_sin, fh, fl, ih, il, v_ref, ya, yb):
@@ -217,37 +239,40 @@
 
 
 def middle_stage(x, ka_cos, ka_sin, q_cos, q_sin, tables):
-    devices, _, count, cols = x.shape
-    rows = 8
+    devices, classes, _, count, cols = x.shape
+    rows = MIDDLE_ROWS
+    blocks = count // rows
     whole = lambda t: pl.BlockSpec(t.shape, lambda i: (0, 0))
     q_spec = pl.BlockSpec((rows, cols), lambda i: (i, 0))
     return pl.pallas_call(
         functools.partial(middle_kernel, devices),
-        grid=(count // rows,),
+        grid=(classes * blocks,),
         in_specs=[
-            pl.BlockSpec((devices, 4, rows, cols), lambda i: (0, 0, i, 0)),
+            pl.BlockSpec((devices, None, 4, rows, cols), lambda i: (0, i // blocks, 0, i % blocks, 0)),
             whole(ka_cos),
             whole(ka_sin),
             q_spec,
             q_spec,
         ]
         + [whole(t) for t in tables],
-        out_specs=pl.BlockSpec((devices, 2, rows, cols), lambda i: (0, 0, i, 0)),
-        out_shape=jax.ShapeDtypeStruct((devices, 2, count, cols), F32),
+        out_specs=pl.BlockSpec((devices, None, 2, rows, cols), lambda i: (0, i // blocks, 0, i % blocks, 0)),
+        out_shape=jax.ShapeDtypeStruct((devices, classes, 2, count, cols), F32),
         scratch_shapes=[pltpu.VMEM((devices * rows, 2 * cols), F32)] * 2,
         cost_estimate=pl.CostEstimate(
-            flops=36 * devices * count * cols * cols * 4, bytes_accessed=24 * devices * count * cols, transcendentals=0
+            flops=36 * devices * classes * count * cols * cols * 4, bytes_accessed=24 * devices * classes * count * cols, transcendentals=0
         ),
         name="middle_stage",
     )(x, ka_cos, ka_sin, q_cos, q_sin, *tables)
 
 
-def tail_kernel(outer, chunk, steps, v_ref, table_ref, cos_ref, sin_ref, *refs):
+def tail_kernel(outer, classes, chunks, steps, v_ref, table_ref, cos_ref, sin_ref, *refs):
     *others, out_ref, rows_ref, high_ref, low_ref = refs
-    chunks = len(others) + 1
     step = pl.program_id(0)
-    count, cols, _ = rows_ref.shape
-    group = min(v_ref.shape[0], 4)
+    _, cols, _ = rows_ref.shape
+    count = outer // chunks
+    pieces = INNER // v_ref.shape[2]
+    block = v_ref.shape[0] // pieces
+    group = min(block, 4)
 
     @pl.when(step == 0)
     def _():
@@ -256,18 +281,19 @@
     @pl.when(step < steps)
     def _():
         table = (high_ref[...], low_ref[...])
-        @pl.loop(0, v_ref.shape[0] // group)
+
+        @pl.loop(0, block // group)
         def _(i):
+            def turned(g, part):
+                own = [v_ref[(i * group + g) * pieces + p, part] for p in range(pieces)]
+                return (own[0] if pieces == 1 else jnp.concatenate(own, axis=0)).T
+
             stacked = jnp.concatenate(
-                [
-                    jnp.concatenate([v_ref[i * group + g, p].T for p in (0, 1)], axis=1)
-                    for g in range(group)
-                ],
-                axis=0,
+                [jnp.concatenate([turned(g, 0), turned(g, 1)], axis=1) for g in range(group)], axis=0
             )
             result = three_dot(split(stacked), table, ((1,), (0,)))
             for g in range(group):
-                j = step * v_ref.shape[0] + i * group + g
+                j = step * block + i * group + g
                 part = result[g * cols : (g + 1) * cols]
                 turn = (cos_ref[pl.ds(j, 1), :], sin_ref[pl.ds(j, 1), :])
                 re, im = times((part[:, :INNER], part[:, INNER:]), turn)
@@ -282,14 +308,24 @@
         def _(i):
             own = pl.ds(pl.multiple_of(i * SUBLANES, SUBLANES), SUBLANES)
             at = pl.ds(pl.multiple_of((step - steps) * tile_rows + i * SUBLANES, SUBLANES), SUBLANES)
-            result = fft_list([(rows_ref[j, at, :INNER], rows_ref[j, at, INNER:]) for j in range(count)], 1)
+            mine = []
+            for n, chunk in enumerate(classes):
+                spectrum = [
+                    (rows_ref[n * count + e, at, :INNER], rows_ref[n * count + e, at, INNER:]) for e in range(count)
+                ]
+                result = fft_list(spectrum, 1)
+                mine.append([rotate(*result[r], (r * (4 * chunk + 1), 4 * outer)) for r in range(count)])
             for r in range(count):
-                mine = rotate(*result[r], (r * (4 * chunk + 1), 4 * outer))
                 if out_ref.ndim == 3:
-                    out_ref[r, own, :INNER] = mine[0]
-                    out_ref[r, own, INNER:] = mine[1]
+                    for n in range(len(classes)):
+                        out_ref[n * count + r, own, :INNER] = mine[n][r][0]
+                        out_ref[n * count + r, own, INNER:] = mine[n][r][1]
                     continue
-                sums = fft_list([(o[r, own, :INNER], o[r, own, INNER:]) for o in others] + [mine], 1)
+                terms = []
+                for o in others:
+                    for n in range(o.shape[0] // count):
+                        terms.append((o[n * count + r, own, :INNER], o[n * count + r, own, INNER:]))
+                sums = fft_list(terms + [m[r] for m in mine], 1)
                 for s in range(chunks):
                     re, im = rotate(*sums[s], (s, 4 * chunks))
                     low = (r + s * count) * INNER
@@ -298,39 +334,42 @@
                     out_ref[own, high : high + INNER] = -im
 
 
-def tail_stage(v, table, cos, sin, others, chunk, chunks):
-    count, _, _, cols = v.shape
-    outer = count * chunks
-    group = math.gcd(count, TAIL_GROUP)
+def tail_stage(v, table, cos, sin, others, classes, chunks, outer):
+    devices, _, _, each, cols = v.shape
+    count = outer // chunks
+    pieces = devices // count
+    total = len(classes) * count
+    block = math.gcd(count, TAIL_GROUP)
+    blocks = count // block
     tile_rows = min(cols, TAIL_ROWS)
     width = 2 * INNER
-    steps = count // group
-    final = chunk == chunks - 1
+    steps = len(classes) * blocks
+    now = lambda i: jnp.minimum(i, steps - 1)
     later = lambda i: jnp.maximum(i - steps, 0)
-    turns_spec = pl.BlockSpec((count, INNER), lambda i: (0, 0))
-    row_spec = pl.BlockSpec((count, tile_rows, width), lambda i: (0, later(i), 0))
-    if final:
+    whole = lambda t: pl.BlockSpec(t.shape, lambda i: (0, 0))
+    row_spec = lambda n: pl.BlockSpec((n, tile_rows, width), lambda i: (0, later(i), 0))
+    if classes[-1] == chunks - 1:
         out_spec = pl.BlockSpec((tile_rows, outer * width), lambda i: (later(i), 0))
         out_shape = jax.ShapeDtypeStruct((cols, outer * width), F32)
     else:
-        out_spec = row_spec
-        out_shape = jax.ShapeDtypeStruct((count, cols, width), F32)
-    others = others if final else []
+        others = []
+        out_spec = row_spec(total)
+        out_shape = jax.ShapeDtypeStruct((total, cols, width), F32)
     return pl.pallas_call(
-        functools.partial(tail_kernel, outer, chunk, steps),
+        functools.partial(tail_kernel, outer, classes, chunks, steps),
         grid=(steps + cols // tile_rows,),
         in_specs=[
-            pl.BlockSpec((group, 2, INNER, cols), lambda i: (jnp.minimum(i, steps - 1), 0, 0, 0)),
-            pl.BlockSpec((width, width), lambda i: (0, 0)),
-            turns_spec,
-            turns_spec,
+            pl.BlockSpec((block * pieces, None, 2, each, cols), lambda i: (now(i) % blocks, now(i) // blocks, 0, 0, 0)),
+            whole(table),
+            whole(cos),
+            whole(sin),
         ]
-        + [row_spec] * len(others),
+        + [row_spec(o.shape[0]) for o in others],
         out_specs=out_spec,
         out_shape=out_shape,
-        scratch_shapes=[pltpu.VMEM((count, cols, width), F32)] + [pltpu.VMEM((width, width), BF16)] * 2,
+        scratch_shapes=[pltpu.VMEM((total, cols, width), F32)] + [pltpu.VMEM((width, width), BF16)] * 2,
         cost_estimate=pl.CostEstimate(
-            flops=6 * count * cols * width * width, bytes_accessed=16 * count * cols * width, transcendentals=0
+            flops=6 * total * cols * width * width, bytes_accessed=16 * total * cols * width, transcendentals=0
         ),
         name="tail_stage",
     )(v, table, cos, sin, *others)
@@ -362,11 +401,14 @@
     return jnp.cos(angle)
 
 
-def spectral_turns(local, cols, devices, device, outer, total):
-    shape = (local, cols)
-    at = iota(shape, 0) + device * local
-    freq = at // INNER + outer * (at % INNER)
-    return turns(iota(shape, 1) * (4 * freq + 1), total)
+def spectral_turns(cols, devices, device, outer, classes, chunks, total):
+    pieces = devices * chunks // outer
+    each = INNER // pieces
+    shape = (len(classes) * each, cols)
+    row = iota(shape, 0)
+    first = chunks * (device // pieces) + classes[0] + row // each
+    inner = (device % pieces) * each + row % each
+    return turns(iota(shape, 1) * (4 * (first + outer * inner) + 1), total)
 
 
 def np_split(value):
@@ -396,34 +438,24 @@
     outer = length // INNER
     total = length * cols * devices
     scale = 1.0 / (total * DIGIT_VAR * math.sqrt(total))
-    chunks = max(1, outer // devices)
-    pieces = max(1, devices // outer)
-    local = length // devices
-    rows = [row_turns(outer, devices, device, h, chunks) for h in range(chunks)]
-    table = row_table(devices, device)
+    chunks = max(1, 2 * outer // devices)
+    groups = [list(range(1)), list(range(1, chunks))] if chunks > 1 else [[0]]
     ka_cos, ka_sin, tables = column_tables(cols, devices, scale)
-    q_cos, q_sin = spectral_turns(local, cols, devices, device, outer, 4 * total)
-    each = local // chunks
 
     arrived = []
-    for h in range(chunks):
-        x = head_stage(limbs_a, limbs_b, *rows[h], table, h, chunks)
-        if pieces > 1:
-            x = x.reshape(outer, 4, pieces, each, cols).transpose(0, 2, 1, 3, 4)
-            x = x.reshape(devices, 4, each, cols)
+    for classes in groups:
+        x = head_stage(limbs_a, limbs_b, device.reshape(1), devices, classes, chunks)
         arrived.append(exchange(x))
     back = []
-    for h in range(chunks):
-        part = slice(h * each, (h + 1) * each)
-        v = middle_stage(arrived[h], ka_cos, ka_sin, q_cos[part], q_sin[part], tables)
-        back.append(exchange(v))
+    for x, classes in zip(arrived, groups):
+        q_cos, q_sin = spectral_turns(cols, devices, device, outer, classes, chunks, 4 * total)
+        back.append(exchange(middle_stage(x, ka_cos, ka_sin, q_cos, q_sin, tables)))
+    table = row_table(devices, device)
     parts = []
-    for h in range(chunks):
-        v = back[h]
-        if pieces > 1:
-            v = v.reshape(outer, pieces, 2, each, cols).transpose(0, 2, 1, 3, 4)
-            v = v.reshape(outer, 2, INNER, cols)
-        parts.append(tail_stage(v, table, *rows[h], parts, h, chunks))
+    for v, classes in zip(back, groups):
+        rows = [row_turns(outer, devices, device, h, chunks) for h in classes]
+        cos, sin = (jnp.concatenate(r, axis=0) for r in zip(*rows))
+        parts.append(tail_stage(v, table, cos, sin, parts, classes, chunks, outer))
     return parts[-1]
 
 

time: 613 us -> 610 us (level)
  waiting for transfers between devices: 494 us -> 486 us
    all_to_all x4, waiting for transfers between devices: 494 us -> 486 us  [exchange(): return lax.all_to_all(value, AXES, split_axis=0, concat_axis=0, tiled=True)]
  transfers between devices with their start and end apart: 4 -> 4, of which waited for: 4 -> 4; matrix products, arithmetic and copies ran while one was open for 0% -> 1% of each run, Pallas kernels for 10% -> 11%
where the time goes in v4:
time: 610 us; the launch traced here: 608 us
  waiting for transfers between devices  486 us (80%)
  Pallas kernels  94.7 us (16%)
  starting transfers between devices  20.8 us (3%)
    all_to_all x4, waiting for transfers between devices, exchange(): return lax.all_to_all(value, AXES, split_axis=0, concat_axis=0, tiled=True)  486 us
    pallas_call x2, Pallas kernels, head_stage(): pl.pallas_call(functools.partial(head_kernel, outer, classes, chunks, ste...  39.6 us
    pallas_call x2, Pallas kernels, middle_stage(): pl.pallas_call(functools.partial(middle_kernel, devices), grid=(classes *...  37.1 us
    all_to_all x4, starting transfers between devices, exchange(): return lax.all_to_all(value, AXES, split_axis=0, concat_axis=0, tiled=True)  20.8 us
    pallas_call x2, Pallas kernels, tail_stage(): pl.pallas_call(functools.partial(tail_kernel, outer, classes, chunks, ste...  18 us
  transfers between devices with their start and end apart: 4, of which 4 were waited for; matrix products, arithmetic and copies ran while one was open for 1% of the time, Pallas kernels for 11%

profile of v4, /device:TPU:0, one launch (start us, length us, event | category | flops | bytes accessed | tf_op | source)
XLA Modules:
  0.0 608.4 jit_solution(9907950275895192222)
XLA Ops:
  0.0 12.5 %head_stage.3 = f32[32,1,4,64,128]{4,3,2,1,0:T(8,128)} custom-call(s32[1]{0:T(128)} %bitcast.device_ref, s32[128,8192]{1,0:T(8,128)} %a_ref.3, s32[128,8192]{1,0:T(8,128)} %b_ref.3), custom_call_target="tpu_custom_call" | custom-call | flops 1610612736 | bytes 8388608 | tf_op jit(solution)/shard_map/head_stage/pallas_call | solution.py:193
  12.5 7.5 %all-to-all-start.2 = ((f32[32,1,4,64,128]{4,3,2,1,0:T(8,128)}), f32[32,1,4,64,128]{4,3,2,1,0:T(8,128)}, u32[]{:S(2)}, u32[]{:S(2)}) async-start(f32[32,1,4,64,128]{4,3,2,1,0:T(8,128)} %head_stage.3), calls=%async_computation.2 | async-start | bytes 8388608 | tf_op jit(solution)/shard_map/all_to_all | solution.py:431
  20.0 27.1 %head_stage.2 = f32[32,3,4,64,128]{4,3,2,1,0:T(8,128)} custom-call(s32[1]{0:T(128)} %bitcast.device_ref, s32[128,8192]{1,0:T(8,128)} %a_ref.3, s32[128,8192]{1,0:T(8,128)} %b_ref.3), custom_call_target="tpu_custom_call" | custom-call | flops 4831838208 | bytes 25165824 | tf_op jit(solution)/shard_map/head_stage/pallas_call | solution.py:193
  47.1 66.8 %all-to-all-done.2.x_ref = f32[32,1,4,64,128]{4,3,2,1,0:T(8,128)} async-done(((f32[32,1,4,64,128]{4,3,2,1,0:T(8,128)}), f32[32,1,4,64,128]{4,3,2,1,0:T(8,128)}, u32[]{:S(2)}, u32[]{:S(2)}) %all-to-all-start.2) | async-done | bytes 4194336 | tf_op jit(solution)/shard_map/all_to_all | solution.py:431
  113.8 3.8 all-to-all-start
  117.7 0.9 fusion.12
  118.5 10.1 %middle_stage.3 = f32[32,1,2,64,128]{4,3,2,1,0:T(8,128)} custom-call(f32[32,1,4,64,128]{4,3,2,1,0:T(8,128)} %all-to-all-done.2.x_ref, f32[32,128]{1,0:T(8,128)} %constant.225.clone.ka_cos, f32[32,128]{1,0:T(8,128)} %constant.226.clone.ka_sin, f32[64,128]{1,0:T(8,128)} %get-tuple-element.8.q_cos, f32[64,128]{1,0:T(8,128)} %get-tuple-element.7.q_sin, ...), custom_call_target="tpu_custom_call" | custom-call | flops 4831838208 | bytes 6291456 | tf_op jit(solution)/shard_map/middle_stage/pallas_call | solution.py:247
  128.7 267.2 %all-to-all-done.x_ref = f32[32,3,4,64,128]{4,3,2,1,0:T(8,128)} async-done(((f32[32,3,4,64,128]{4,3,2,1,0:T(8,128)}), f32[32,3,4,64,128]{4,3,2,1,0:T(8,128)}, u32[]{:S(2)}, u32[]{:S(2)}) %all-to-all-start) | async-done | bytes 12582944 | tf_op jit(solution)/shard_map/all_to_all | solution.py:431
  395.9 5.8 all-to-all-start.3
  401.7 1.3 fusion.7
  402.9 27.0 %middle_stage.2 = f32[32,3,2,64,128]{4,3,2,1,0:T(8,128)} custom-call(f32[32,3,4,64,128]{4,3,2,1,0:T(8,128)} %all-to-all-done.x_ref, f32[32,128]{1,0:T(8,128)} %constant.225.clone.ka_cos, f32[32,128]{1,0:T(8,128)} %constant.226.clone.ka_sin, f32[192,128]{1,0:T(8,128)} %get-tuple-element.6.q_cos, f32[192,128]{1,0:T(8,128)} %get-tuple-element.5.q_sin, ...), custom_call_target="tpu_custom_call" | custom-call | flops 14495514624 | bytes 18874368 | tf_op jit(solution)/shard_map/middle_stage/pallas_call | solution.py:247
  429.9 20.4 %all-to-all-done.3.v_ref = f32[32,1,2,64,128]{4,3,2,1,0:T(8,128)S(1)} async-done(((f32[32,1,2,64,128]{4,3,2,1,0:T(8,128)}), f32[32,1,2,64,128]{4,3,2,1,0:T(8,128)S(1)}, u32[]{:S(2)}, u32[]{:S(2)}) %all-to-all-start.3) | async-done | bytes 2097184 | tf_op jit(solution)/shard_map/all_to_all | solution.py:431
  450.3 0.0 copy-start
  450.3 1.4 copy-done
  451.7 3.8 all-to-all-start.1
  455.5 0.8 fusion.26
  456.4 0.6 pad_maximum_fusion
  457.0 2.0 fusion.3.table_ref
  459.0 5.2 tail_stage.2.refs_0_
  464.2 131.4 %all-to-all-done.1.v_ref = f32[32,3,2,64,128]{4,3,2,1,0:T(8,128)} async-done(((f32[32,3,2,64,128]{4,3,2,1,0:T(8,128)}), f32[32,3,2,64,128]{4,3,2,1,0:T(8,128)}, u32[]{:S(2)}, u32[]{:S(2)}) %all-to-all-start.1) | async-done | bytes 6291488 | tf_op jit(solution)/shard_map/all_to_all | solution.py:431
  595.5 12.8 %tail_stage.3 = f32[128,16384]{1,0:T(8,128)} custom-call(f32[32,3,2,64,128]{4,3,2,1,0:T(8,128)} %all-to-all-done.1.v_ref, f32[256,256]{1,0:T(8,128)} %fusion.3.table_ref, f32[48,128]{1,0:T(8,128)} %get-tuple-element.35.cos_ref, f32[48,128]{1,0:T(8,128)} %get-tuple-element.36.sin_ref, f32[16,128,256]{2,1,0:T(8,128)} %tail_stage.2.refs_0_), custom_call_target="tpu_custom_call" | custom-call | flops 2415919104 | bytes 25165824 | tf_op jit(solution)/shard_map/tail_stage/pallas_call | solution.py:358
  (14 shorter events, 0.1 us)
Async XLA Ops:
  12.5 101.3 %all-to-all-start.2 = ((f32[32,1,4,64,128]{4,3,2,1,0:T(8,128)}), f32[32,1,4,64,128]{4,3,2,1,0:T(8,128)}, u32[]{:S(2)}, u32[]{:S(2)}) async-start(f32[32,1,4,64,128]{4,3,2,1,0:T(8,128)} %head_stage.3), calls=%async_computation.2 | async-start | bytes 8388608 | tf_op jit(solution)/shard_map/all_to_all | solution.py:431
  113.8 282.0 %all-to-all-start = ((f32[32,3,4,64,128]{4,3,2,1,0:T(8,128)}), f32[32,3,4,64,128]{4,3,2,1,0:T(8,128)}, u32[]{:S(2)}, u32[]{:S(2)}) async-start(f32[32,3,4,64,128]{4,3,2,1,0:T(8,128)} %head_stage.2), calls=%async_computation | async-start | bytes 25165824 | tf_op jit(solution)/shard_map/all_to_all | solution.py:431
  395.9 54.5 %all-to-all-start.3 = ((f32[32,1,2,64,128]{4,3,2,1,0:T(8,128)}), f32[32,1,2,64,128]{4,3,2,1,0:T(8,128)S(1)}, u32[]{:S(2)}, u32[]{:S(2)}) async-start(f32[32,1,2,64,128]{4,3,2,1,0:T(8,128)} %middle_stage.3), calls=%async_computation.3 | async-start | bytes 4194304 | tf_op jit(solution)/shard_map/all_to_all | solution.py:431
  450.3 1.4 copy-start
  451.7 143.8 %all-to-all-start.1 = ((f32[32,3,2,64,128]{4,3,2,1,0:T(8,128)}), f32[32,3,2,64,128]{4,3,2,1,0:T(8,128)}, u32[]{:S(2)}, u32[]{:S(2)}) async-start(f32[32,3,2,64,128]{4,3,2,1,0:T(8,128)} %middle_stage.2), calls=%async_computation.1 | async-start | bytes 12582912 | tf_op jit(solution)/shard_map/all_to_all | solution.py:431

commit v5 on v4

--- a/solution.py
+++ b/solution.py
@@ -17,6 +17,7 @@
 TAIL_ROWS = 64
 TAIL_GROUP = 16
 MIDDLE_ROWS = 8
+VMEM_BYTES = 67043328
 AXES = ("fft", "grp")
 BF16 = jnp.bfloat16
 F32 = jnp.float32
@@ -202,6 +203,7 @@
         cost_estimate=pl.CostEstimate(
             flops=12 * total * cols * width * width, bytes_accessed=16 * total * cols * width, transcendentals=0
         ),
+        compiler_params=pltpu.CompilerParams(vmem_limit_bytes=VMEM_BYTES),
         name="head_stage",
     )(device, limbs_a, limbs_b)
 
@@ -261,6 +263,7 @@
         cost_estimate=pl.CostEstimate(
             flops=36 * devices * classes * count * cols * cols * 4, bytes_accessed=24 * devices * classes * count * cols, transcendentals=0
         ),
+        compiler_params=pltpu.CompilerParams(vmem_limit_bytes=VMEM_BYTES),
         name="middle_stage",
     )(x, ka_cos, ka_sin, q_cos, q_sin, *tables)
 
@@ -371,12 +374,13 @@
         cost_estimate=pl.CostEstimate(
             flops=6 * total * cols * width * width, bytes_accessed=16 * total * cols * width, transcendentals=0
         ),
+        compiler_params=pltpu.CompilerParams(vmem_limit_bytes=VMEM_BYTES),
         name="tail_stage",
     )(v, table, cos, sin, *others)
 
 
 def turns(phase, modulus):
-    angle = (phase % modulus).astype(F32) * (2.0 * math.pi / modulus)
+    angle = (phase & (modulus - 1)).astype(F32) * (2.0 * math.pi / modulus)
     return (jnp.cos(angle), jnp.sin(angle))
 
 
@@ -395,9 +399,10 @@
     shape = (2 * INNER, 2 * INNER)
     row, col = (iota(shape, 0), iota(shape, 1))
     modulus = 4 * INNER * devices
-    phase = 4 * (row % INNER) * (devices * (col % INNER) + device)
-    quarter = INNER * devices * (row // INNER - col // INNER)
-    angle = ((phase + quarter) % modulus).astype(F32) * (2.0 * math.pi / modulus)
+    mask = INNER - 1
+    phase = 4 * (row & mask) * (devices * (col & mask) + device)
+    quarter = devices * ((row & INNER) - (col & INNER))
+    angle = ((phase + quarter) & (modulus - 1)).astype(F32) * (2.0 * math.pi / modulus)
     return jnp.cos(angle)
 
 

time: 610 us -> 608 us (level)
  no operation moved by 1% of the time
where the time goes in v5:
time: 608 us; the launch traced here: 607 us
  waiting for transfers between devices  486 us (80%)
  Pallas kernels  94.6 us (16%)
  starting transfers between devices  20.9 us (3%)
    all_to_all x4, waiting for transfers between devices, exchange(): return lax.all_to_all(value, AXES, split_axis=0, concat_axis=0, tiled=True)  486 us
    pallas_call x2, Pallas kernels, head_stage(): pl.pallas_call(functools.partial(head_kernel, outer, classes, chunks, ste...  39.4 us
    pallas_call x2, Pallas kernels, middle_stage(): pl.pallas_call(functools.partial(middle_kernel, devices), grid=(classes *...  37.1 us
    all_to_all x4, starting transfers between devices, exchange(): return lax.all_to_all(value, AXES, split_axis=0, concat_axis=0, tiled=True)  20.9 us
    pallas_call x2, Pallas kernels, tail_stage(): pl.pallas_call(functools.partial(tail_kernel, outer, classes, chunks, ste...  18 us
  transfers between devices with their start and end apart: 4, of which 4 were waited for; matrix products, arithmetic and copies ran while one was open for 1% of the time, Pallas kernels for 11%

profile of v5, /device:TPU:0, one launch (start us, length us, event | category | flops | bytes accessed | tf_op | source)
XLA Modules:
  0.0 607.0 jit_solution(9216911349596452625)
XLA Ops:
  0.0 12.4 %head_stage.3 = f32[32,1,4,64,128]{4,3,2,1,0:T(8,128)} custom-call(s32[1]{0:T(128)} %bitcast.device_ref, s32[128,8192]{1,0:T(8,128)} %a_ref.3, s32[128,8192]{1,0:T(8,128)} %b_ref.3), custom_call_target="tpu_custom_call" | custom-call | flops 1610612736 | bytes 8388608 | tf_op jit(solution)/shard_map/head_stage/pallas_call | solution.py:194
  12.4 7.5 %all-to-all-start.2 = ((f32[32,1,4,64,128]{4,3,2,1,0:T(8,128)}), f32[32,1,4,64,128]{4,3,2,1,0:T(8,128)}, u32[]{:S(2)}, u32[]{:S(2)}) async-start(f32[32,1,4,64,128]{4,3,2,1,0:T(8,128)} %head_stage.3), calls=%async_computation.2 | async-start | bytes 8388608 | tf_op jit(solution)/shard_map/all_to_all | solution.py:436
  19.9 27.0 %head_stage.2 = f32[32,3,4,64,128]{4,3,2,1,0:T(8,128)} custom-call(s32[1]{0:T(128)} %bitcast.device_ref, s32[128,8192]{1,0:T(8,128)} %a_ref.3, s32[128,8192]{1,0:T(8,128)} %b_ref.3), custom_call_target="tpu_custom_call" | custom-call | flops 4831838208 | bytes 25165824 | tf_op jit(solution)/shard_map/head_stage/pallas_call | solution.py:194
  46.9 66.8 %all-to-all-done.2.x_ref = f32[32,1,4,64,128]{4,3,2,1,0:T(8,128)} async-done(((f32[32,1,4,64,128]{4,3,2,1,0:T(8,128)}), f32[32,1,4,64,128]{4,3,2,1,0:T(8,128)}, u32[]{:S(2)}, u32[]{:S(2)}) %all-to-all-start.2) | async-done | bytes 4194336 | tf_op jit(solution)/shard_map/all_to_all | solution.py:436
  113.7 3.8 all-to-all-start
  117.6 0.9 fusion.2
  118.5 10.2 %middle_stage.3 = f32[32,1,2,64,128]{4,3,2,1,0:T(8,128)} custom-call(f32[32,1,4,64,128]{4,3,2,1,0:T(8,128)} %all-to-all-done.2.x_ref, f32[32,128]{1,0:T(8,128)} %constant.138.clone.ka_cos, f32[32,128]{1,0:T(8,128)} %constant.139.clone.ka_sin, f32[64,128]{1,0:T(8,128)} %get-tuple-element.8.q_cos, f32[64,128]{1,0:T(8,128)} %get-tuple-element.7.q_sin, ...), custom_call_target="tpu_custom_call" | custom-call | flops 4831838208 | bytes 6291456 | tf_op jit(solution)/shard_map/middle_stage/pallas_call | solution.py:249
  128.6 267.2 %all-to-all-done.x_ref = f32[32,3,4,64,128]{4,3,2,1,0:T(8,128)} async-done(((f32[32,3,4,64,128]{4,3,2,1,0:T(8,128)}), f32[32,3,4,64,128]{4,3,2,1,0:T(8,128)}, u32[]{:S(2)}, u32[]{:S(2)}) %all-to-all-start) | async-done | bytes 12582944 | tf_op jit(solution)/shard_map/all_to_all | solution.py:436
  395.8 5.9 all-to-all-start.3
  401.7 1.2 fusion
  402.9 27.0 %middle_stage.2 = f32[32,3,2,64,128]{4,3,2,1,0:T(8,128)} custom-call(f32[32,3,4,64,128]{4,3,2,1,0:T(8,128)} %all-to-all-done.x_ref, f32[32,128]{1,0:T(8,128)} %constant.138.clone.ka_cos, f32[32,128]{1,0:T(8,128)} %constant.139.clone.ka_sin, f32[192,128]{1,0:T(8,128)} %get-tuple-element.6.q_cos, f32[192,128]{1,0:T(8,128)} %get-tuple-element.5.q_sin, ...), custom_call_target="tpu_custom_call" | custom-call | flops 14495514624 | bytes 18874368 | tf_op jit(solution)/shard_map/middle_stage/pallas_call | solution.py:249
  429.9 20.5 %all-to-all-done.3.v_ref = f32[32,1,2,64,128]{4,3,2,1,0:T(8,128)} async-done(((f32[32,1,2,64,128]{4,3,2,1,0:T(8,128)}), f32[32,1,2,64,128]{4,3,2,1,0:T(8,128)}, u32[]{:S(2)}, u32[]{:S(2)}) %all-to-all-start.3) | async-done | bytes 2097184 | tf_op jit(solution)/shard_map/all_to_all | solution.py:436
  450.3 3.8 all-to-all-start.1
  454.2 0.8 fusion.4
  455.0 0.6 pad_maximum_fusion
  455.6 1.7 multiply_cosine_fusion.table_ref
  457.3 5.2 tail_stage.2.refs_0_
  462.5 131.7 %all-to-all-done.1.v_ref = f32[32,3,2,64,128]{4,3,2,1,0:T(8,128)} async-done(((f32[32,3,2,64,128]{4,3,2,1,0:T(8,128)}), f32[32,3,2,64,128]{4,3,2,1,0:T(8,128)}, u32[]{:S(2)}, u32[]{:S(2)}) %all-to-all-start.1) | async-done | bytes 6291488 | tf_op jit(solution)/shard_map/all_to_all | solution.py:436
  594.2 12.8 %tail_stage.3 = f32[128,16384]{1,0:T(8,128)} custom-call(f32[32,3,2,64,128]{4,3,2,1,0:T(8,128)} %all-to-all-done.1.v_ref, f32[256,256]{1,0:T(8,128)} %multiply_cosine_fusion.table_ref, f32[48,128]{1,0:T(8,128)} %get-tuple-element.31.cos_ref, f32[48,128]{1,0:T(8,128)} %get-tuple-element.32.sin_ref, f32[16,128,256]{2,1,0:T(8,128)} %tail_stage.2.refs_0_), custom_call_target="tpu_custom_call" | custom-call | flops 2415919104 | bytes 25165824 | tf_op jit(solution)/shard_map/tail_stage/pallas_call | solution.py:361
  (13 shorter events, 0.1 us)
Async XLA Ops:
  12.4 101.3 %all-to-all-start.2 = ((f32[32,1,4,64,128]{4,3,2,1,0:T(8,128)}), f32[32,1,4,64,128]{4,3,2,1,0:T(8,128)}, u32[]{:S(2)}, u32[]{:S(2)}) async-start(f32[32,1,4,64,128]{4,3,2,1,0:T(8,128)} %head_stage.3), calls=%async_computation.2 | async-start | bytes 8388608 | tf_op jit(solution)/shard_map/all_to_all | solution.py:436
  113.7 282.0 %all-to-all-start = ((f32[32,3,4,64,128]{4,3,2,1,0:T(8,128)}), f32[32,3,4,64,128]{4,3,2,1,0:T(8,128)}, u32[]{:S(2)}, u32[]{:S(2)}) async-start(f32[32,3,4,64,128]{4,3,2,1,0:T(8,128)} %head_stage.2), calls=%async_computation | async-start | bytes 25165824 | tf_op jit(solution)/shard_map/all_to_all | solution.py:436
  395.8 54.5 %all-to-all-start.3 = ((f32[32,1,2,64,128]{4,3,2,1,0:T(8,128)}), f32[32,1,2,64,128]{4,3,2,1,0:T(8,128)}, u32[]{:S(2)}, u32[]{:S(2)}) async-start(f32[32,1,2,64,128]{4,3,2,1,0:T(8,128)} %middle_stage.3), calls=%async_computation.3 | async-start | bytes 4194304 | tf_op jit(solution)/shard_map/all_to_all | solution.py:436
  450.3 143.8 %all-to-all-start.1 = ((f32[32,3,2,64,128]{4,3,2,1,0:T(8,128)}), f32[32,3,2,64,128]{4,3,2,1,0:T(8,128)}, u32[]{:S(2)}, u32[]{:S(2)}) async-start(f32[32,3,2,64,128]{4,3,2,1,0:T(8,128)} %middle_stage.2), calls=%async_computation.1 | async-start | bytes 12582912 | tf_op jit(solution)/shard_map/all_to_all | solution.py:436

commit v6 on v5

--- a/solution.py
+++ b/solution.py
@@ -140,7 +140,7 @@
     def _():
         tile_rows = a_ref.shape[0]
 
-        @pl.loop(0, tile_rows // SUBLANES)
+        @pl.loop(0, tile_rows // SUBLANES, unroll=2)
         def _(i):
             own = pl.ds(pl.multiple_of(i * SUBLANES, SUBLANES), SUBLANES)
             for side, src in ((0, a_ref), (cols, b_ref)):
@@ -157,7 +157,7 @@
     def _():
         table = (high_ref[...], low_ref[...])
 
-        @pl.loop(0, group)
+        @pl.loop(0, group, unroll=4)
         def _(g):
             j = (step - steps) * group + g
             if cols % INNER == 0:
@@ -285,7 +285,7 @@
     def _():
         table = (high_ref[...], low_ref[...])
 
-        @pl.loop(0, block // group)
+        @pl.loop(0, block // group, unroll=4)
         def _(i):
             def turned(g, part):
                 own = [v_ref[(i * group + g) * pieces + p, part] for p in range(pieces)]
@@ -307,7 +307,7 @@
     def _():
         tile_rows = out_ref.shape[-2]
 
-        @pl.loop(0, tile_rows // SUBLANES)
+        @pl.loop(0, tile_rows // SUBLANES, unroll=2)
         def _(i):
             own = pl.ds(pl.multiple_of(i * SUBLANES, SUBLANES), SUBLANES)
             at = pl.ds(pl.multiple_of((step - steps) * tile_rows + i * SUBLANES, SUBLANES), SUBLANES)

time: 608 us -> 605 us (level)
  Pallas kernels: 94.6 us -> 84.8 us
  waiting for transfers between devices: 486 us -> 493 us
    pallas_call x2, Pallas kernels: 39.4 us -> 31.4 us  [head_stage(): pl.pallas_call(functools.partial(head_kernel, outer, classes, chunks, ste...]
    all_to_all x4, waiting for transfers between devices: 486 us -> 493 us  [exchange(): return lax.all_to_all(value, AXES, split_axis=0, concat_axis=0, tiled=True)]
  transfers between devices with their start and end apart: 4 -> 4, of which waited for: 4 -> 4; matrix products, arithmetic and copies ran while one was open for 1% -> 1% of each run, Pallas kernels for 11% -> 10%
where the time goes in v6:
time: 605 us; the launch traced here: 604 us
  waiting for transfers between devices  493 us (81%)
  Pallas kernels  84.8 us (14%)
  starting transfers between devices  20.9 us (3%)
    all_to_all x4, waiting for transfers between devices, exchange(): return lax.all_to_all(value, AXES, split_axis=0, concat_axis=0, tiled=True)  493 us
    pallas_call x2, Pallas kernels, middle_stage(): pl.pallas_call(functools.partial(middle_kernel, devices), grid=(classes *...  37.1 us
    pallas_call x2, Pallas kernels, head_stage(): pl.pallas_call(functools.partial(head_kernel, outer, classes, chunks, ste...  31.4 us
    all_to_all x4, starting transfers between devices, exchange(): return lax.all_to_all(value, AXES, split_axis=0, concat_axis=0, tiled=True)  20.9 us
    pallas_call x2, Pallas kernels, tail_stage(): pl.pallas_call(functools.partial(tail_kernel, outer, classes, chunks, ste...  16.3 us
  transfers between devices with their start and end apart: 4, of which 4 were waited for; matrix products, arithmetic and copies ran while one was open for 1% of the time, Pallas kernels for 10%

profile of v6, /device:TPU:0, one launch (start us, length us, event | category | flops | bytes accessed | tf_op | source)
XLA Modules:
  0.0 603.6 jit_solution(10889810692817764431)
XLA Ops:
  0.0 10.2 %head_stage.3 = f32[32,1,4,64,128]{4,3,2,1,0:T(8,128)} custom-call(s32[1]{0:T(128)} %bitcast.device_ref, s32[128,8192]{1,0:T(8,128)} %a_ref.3, s32[128,8192]{1,0:T(8,128)} %b_ref.3), custom_call_target="tpu_custom_call" | custom-call | flops 1610612736 | bytes 8388608 | tf_op jit(solution)/shard_map/head_stage/pallas_call | solution.py:194
  10.2 7.5 %all-to-all-start.2 = ((f32[32,1,4,64,128]{4,3,2,1,0:T(8,128)}), f32[32,1,4,64,128]{4,3,2,1,0:T(8,128)}, u32[]{:S(2)}, u32[]{:S(2)}) async-start(f32[32,1,4,64,128]{4,3,2,1,0:T(8,128)} %head_stage.3), calls=%async_computation.2 | async-start | bytes 8388608 | tf_op jit(solution)/shard_map/all_to_all | solution.py:436
  17.7 21.2 %head_stage.2 = f32[32,3,4,64,128]{4,3,2,1,0:T(8,128)} custom-call(s32[1]{0:T(128)} %bitcast.device_ref, s32[128,8192]{1,0:T(8,128)} %a_ref.3, s32[128,8192]{1,0:T(8,128)} %b_ref.3), custom_call_target="tpu_custom_call" | custom-call | flops 4831838208 | bytes 25165824 | tf_op jit(solution)/shard_map/head_stage/pallas_call | solution.py:194
  38.9 72.7 %all-to-all-done.2.x_ref = f32[32,1,4,64,128]{4,3,2,1,0:T(8,128)} async-done(((f32[32,1,4,64,128]{4,3,2,1,0:T(8,128)}), f32[32,1,4,64,128]{4,3,2,1,0:T(8,128)}, u32[]{:S(2)}, u32[]{:S(2)}) %all-to-all-start.2) | async-done | bytes 4194336 | tf_op jit(solution)/shard_map/all_to_all | solution.py:436
  111.5 3.8 all-to-all-start
  115.4 0.9 fusion.2
  116.2 10.2 %middle_stage.3 = f32[32,1,2,64,128]{4,3,2,1,0:T(8,128)} custom-call(f32[32,1,4,64,128]{4,3,2,1,0:T(8,128)} %all-to-all-done.2.x_ref, f32[32,128]{1,0:T(8,128)} %constant.138.clone.ka_cos, f32[32,128]{1,0:T(8,128)} %constant.139.clone.ka_sin, f32[64,128]{1,0:T(8,128)} %get-tuple-element.8.q_cos, f32[64,128]{1,0:T(8,128)} %get-tuple-element.7.q_sin, ...), custom_call_target="tpu_custom_call" | custom-call | flops 4831838208 | bytes 6291456 | tf_op jit(solution)/shard_map/middle_stage/pallas_call | solution.py:249
  126.4 267.2 %all-to-all-done.x_ref = f32[32,3,4,64,128]{4,3,2,1,0:T(8,128)} async-done(((f32[32,3,4,64,128]{4,3,2,1,0:T(8,128)}), f32[32,3,4,64,128]{4,3,2,1,0:T(8,128)}, u32[]{:S(2)}, u32[]{:S(2)}) %all-to-all-start) | async-done | bytes 12582944 | tf_op jit(solution)/shard_map/all_to_all | solution.py:436
  393.6 5.9 all-to-all-start.3
  399.5 1.2 fusion
  400.7 27.0 %middle_stage.2 = f32[32,3,2,64,128]{4,3,2,1,0:T(8,128)} custom-call(f32[32,3,4,64,128]{4,3,2,1,0:T(8,128)} %all-to-all-done.x_ref, f32[32,128]{1,0:T(8,128)} %constant.138.clone.ka_cos, f32[32,128]{1,0:T(8,128)} %constant.139.clone.ka_sin, f32[192,128]{1,0:T(8,128)} %get-tuple-element.6.q_cos, f32[192,128]{1,0:T(8,128)} %get-tuple-element.5.q_sin, ...), custom_call_target="tpu_custom_call" | custom-call | flops 14495514624 | bytes 18874368 | tf_op jit(solution)/shard_map/middle_stage/pallas_call | solution.py:249
  427.7 20.5 %all-to-all-done.3.v_ref = f32[32,1,2,64,128]{4,3,2,1,0:T(8,128)} async-done(((f32[32,1,2,64,128]{4,3,2,1,0:T(8,128)}), f32[32,1,2,64,128]{4,3,2,1,0:T(8,128)}, u32[]{:S(2)}, u32[]{:S(2)}) %all-to-all-start.3) | async-done | bytes 2097184 | tf_op jit(solution)/shard_map/all_to_all | solution.py:436
  448.1 3.8 all-to-all-start.1
  452.0 0.8 fusion.4
  452.8 0.6 pad_maximum_fusion
  453.4 1.7 multiply_cosine_fusion.table_ref
  455.1 4.6 tail_stage.2.refs_0_
  459.7 132.2 %all-to-all-done.1.v_ref = f32[32,3,2,64,128]{4,3,2,1,0:T(8,128)} async-done(((f32[32,3,2,64,128]{4,3,2,1,0:T(8,128)}), f32[32,3,2,64,128]{4,3,2,1,0:T(8,128)}, u32[]{:S(2)}, u32[]{:S(2)}) %all-to-all-start.1) | async-done | bytes 6291488 | tf_op jit(solution)/shard_map/all_to_all | solution.py:436
  592.0 11.6 %tail_stage.3 = f32[128,16384]{1,0:T(8,128)} custom-call(f32[32,3,2,64,128]{4,3,2,1,0:T(8,128)} %all-to-all-done.1.v_ref, f32[256,256]{1,0:T(8,128)} %multiply_cosine_fusion.table_ref, f32[48,128]{1,0:T(8,128)} %get-tuple-element.31.cos_ref, f32[48,128]{1,0:T(8,128)} %get-tuple-element.32.sin_ref, f32[16,128,256]{2,1,0:T(8,128)} %tail_stage.2.refs_0_), custom_call_target="tpu_custom_call" | custom-call | flops 2415919104 | bytes 25165824 | tf_op jit(solution)/shard_map/tail_stage/pallas_call | solution.py:361
  (13 shorter events, 0.1 us)
Async XLA Ops:
  10.2 101.3 %all-to-all-start.2 = ((f32[32,1,4,64,128]{4,3,2,1,0:T(8,128)}), f32[32,1,4,64,128]{4,3,2,1,0:T(8,128)}, u32[]{:S(2)}, u32[]{:S(2)}) async-start(f32[32,1,4,64,128]{4,3,2,1,0:T(8,128)} %head_stage.3), calls=%async_computation.2 | async-start | bytes 8388608 | tf_op jit(solution)/shard_map/all_to_all | solution.py:436
  111.5 282.0 %all-to-all-start = ((f32[32,3,4,64,128]{4,3,2,1,0:T(8,128)}), f32[32,3,4,64,128]{4,3,2,1,0:T(8,128)}, u32[]{:S(2)}, u32[]{:S(2)}) async-start(f32[32,3,4,64,128]{4,3,2,1,0:T(8,128)} %head_stage.2), calls=%async_computation | async-start | bytes 25165824 | tf_op jit(solution)/shard_map/all_to_all | solution.py:436
  393.6 54.5 %all-to-all-start.3 = ((f32[32,1,2,64,128]{4,3,2,1,0:T(8,128)}), f32[32,1,2,64,128]{4,3,2,1,0:T(8,128)}, u32[]{:S(2)}, u32[]{:S(2)}) async-start(f32[32,1,2,64,128]{4,3,2,1,0:T(8,128)} %middle_stage.3), calls=%async_computation.3 | async-start | bytes 4194304 | tf_op jit(solution)/shard_map/all_to_all | solution.py:436
  448.1 143.8 %all-to-all-start.1 = ((f32[32,3,2,64,128]{4,3,2,1,0:T(8,128)}), f32[32,3,2,64,128]{4,3,2,1,0:T(8,128)}, u32[]{:S(2)}, u32[]{:S(2)}) async-start(f32[32,3,2,64,128]{4,3,2,1,0:T(8,128)} %middle_stage.2), calls=%async_computation.1 | async-start | bytes 12582912 | tf_op jit(solution)/shard_map/all_to_all | solution.py:436
